TPU v7x, 128 devices: a whole 4x4x4 slice. The times are simulated.
128 devices in a mesh: comp: 32 (over z, y, core), lat: 4 (over x).
Axes of the slice: x: 4, y: 4, z: 4, core: 2. Of those that a mesh axis runs over, the one named last changes fastest.
Arguments:
- spectrum: float32 [32, 36, 384, 512], P('comp', None, 'lat'), may hold values from 0.1 to 3
- sea_mask: int32 [384, 512], P('lat'), may hold values from 0 to 1, as said below
- point_index: int32 [4, 32768], P('lat'), may hold values from 0 to 49151, as said below
- band_counts: int32 [4], P('lat'), may hold values from 16384 to 32768, as said below
- sub_counts: int32 [32], P('comp'), may hold values from 2 to 4, as said below
- mix_in: bfloat16 [1152, 1152], replicated, may hold values from -0.1875 to 0.1875
- mix_out: bfloat16 [1152, 1152], replicated, may hold values from -0.1875 to 0.1875
- growth: float32 [32, 36], replicated, may hold values from 0.05 to 1
- damping: float32 [32, 36], replicated, may hold values from 0.1 to 2
Outputs:
- new_spectrum: float32 [32, 36, 384, 512], P('comp', None, 'lat')
Inputs may be any that keep to these rules, and one draw needn't show every extreme that they name: `sea_mask`: exactly band_counts[b] of the 49152 cells of band b are sea. `point_index`: row b lists the sea cells of band b in increasing order in its first band_counts[b] slots, zeros after them. `band_counts`: some band has exactly 32768 sea cells. `sub_counts`: some frequency has exactly 4 substeps.
All inputs are finite; a program needn't handle non-finite values.
Results may differ from a plain program's by a relative error of at most 0.0015.
Values may be sent and summed in bfloat16 or wider, within the bound.
A program may use at most 128 MiB of HBM per device.

v0:
```python
import functools
import math

import jax
import jax.numpy as jnp
import numpy as np
from jax import lax
from jax.experimental import pallas as pl
from jax.experimental.pallas import tpu as pltpu
from jax.sharding import PartitionSpec as P

MESH = pl.DeviceIdType.MESH
F32, BF16 = jnp.float32, jnp.bfloat16
NSUB = 4
NDIR, NFREQ, ROWS, LON = 36, 32, 96, 512
K = NDIR * NFREQ
GROUPS = 32
CHUNKS = ROWS // GROUPS
HALO = 4
EDGE = 8
SIDE = ROWS + EDGE
MAIN = 32
MSG = 4 * MAIN + 16
HID = 1184
TILE1 = HID // 2
TILE2 = 512
BLOCK = 8

LATIN = [((i + dy) % 4, dy) for i in range(4) for dy in (1, 3, 2, 0) if ((i + dy) % 4, dy) != (0, 0)]
ORDER = [(dz, dy, dc) for dz, dy in LATIN for dc in (0, 1)] + [(0, 0, 1)]


def direction(quadrant, place):
    return 9 * quadrant + place


def angle_tables():
    main = [direction(q, t) for q in range(4) for t in range(8)]
    left_plus = [direction(i, 8) for _ in range(4) for i in range(2)]
    left_minus = [direction(2 + i, 8) for _ in range(4) for i in range(2)]
    angles = (np.array(main + left_plus + left_minus, np.float32) + np.float32(0.5)) * np.float32(2.0 * np.pi / NDIR)
    table = np.stack([np.abs(np.cos(angles)), np.abs(np.sin(angles))]).astype(np.float32)
    return np.ascontiguousarray(np.broadcast_to(table[:, :, None], (2, 48, 128)))


def natural(c):
    k = c & 31
    main = 36 * (c >> 5) + 9 * (k >> 3) + (k & 7)
    r = c - 1024
    left = 36 * ((r & 63) >> 1) + 9 * (2 * (r & 1) + (r >> 6)) + 8
    return jnp.where(c < 1024, main, left)


def kernel(
    spec, mask, scal, table, w_in, w_out, mean_w, gain, damp,
    out,
    fp, fm, lp, lm, msk, mh, ox, oxm, oy, oym, oxl, oyl, ml,
    pb, rm, ib, ri, win, wout, perm, wi, wo, sq, hq, lf, rl, tl,
    in_sem, halo_send, halo_recv, mask_send, mask_recv, lmask_sem, w_sem, own_sem,
    send_sem, recv_sem, back_send, back_recv, out_sem,
):
    me, lat = lax.axis_index("comp"), lax.axis_index("lat")
    z, y, core = lax.div(me, 8), lax.rem(lax.div(me, 2), 4), lax.rem(me, 2)
    partners = [
        (lax.rem(z + dz, 4) * 4 + lax.rem(y + dy, 4)) * 2 + lax.rem(core + dc, 2) for dz, dy, dc in ORDER
    ]

    for quadrant in range(4):
        dst, base, sem = (fp, EDGE, 0) if quadrant < 2 else (fm, 0, 1)
        for t in range(8):
            slot = 8 * (quadrant % 2) + t
            pltpu.make_async_copy(
                spec.at[0, direction(quadrant, t)], dst.at[pl.ds(base, ROWS), slot, :], in_sem.at[sem]
            ).start()
        dst, sem = (lp, 2) if quadrant < 2 else (lm, 3)
        for ct in range(4):
            pltpu.make_async_copy(
                spec.at[0, direction(quadrant, 8), :, pl.ds(128 * ct, 128)],
                dst.at[pl.ds(base, ROWS), 2 * ct + quadrant % 2, :],
                in_sem.at[sem],
            ).start()
    w_copies = [
        pltpu.make_async_copy(w_in, win, w_sem.at[0]),
        pltpu.make_async_copy(w_out, wout, w_sem.at[1]),
    ]
    for copy in w_copies:
        copy.start()

    barrier = pltpu.get_barrier_semaphore()
    for partner in partners:
        pl.semaphore_signal(barrier, inc=1, device_id=(partner, lat), device_id_type=MESH)
    inner_low, inner_high = lat > 0, lat < 3

    @pl.when(inner_low)
    def _():
        pl.semaphore_signal(barrier, inc=1, device_id=(me, lat - 1), device_id_type=MESH)

    @pl.when(inner_high)
    def _():
        pl.semaphore_signal(barrier, inc=1, device_id=(me, lat + 1), device_id_type=MESH)

    neighbours = jnp.where(inner_low, 1, 0) + jnp.where(inner_high, 1, 0)
    pl.semaphore_wait(barrier, len(ORDER) + neighbours)

    def mask_copy(up):
        return pltpu.make_async_remote_copy(
            mask.at[pl.ds(88, 8)] if up else mask.at[pl.ds(0, 8)],
            mh.at[0 if up else 1],
            mask_send.at[0 if up else 1],
            mask_recv.at[0 if up else 1],
            device_id=(me, lat + 1 if up else lat - 1),
            device_id_type=MESH,
        )

    def halo_copies(up):
        side = 0 if up else 1
        target = (me, lat + 1 if up else lat - 1)
        field, left = (fp, lp) if up else (fm, lm)
        src, dst = (SIDE - HALO, EDGE - HALO) if up else (0, ROWS)
        return [
            pltpu.make_async_remote_copy(
                ref.at[pl.ds(src, HALO)], ref.at[pl.ds(dst, HALO)], halo_send.at[side, i], halo_recv.at[side, i],
                device_id=target, device_id_type=MESH,
            )
            for i, ref in enumerate((field, left))
        ]

    @pl.when(inner_high)
    def _():
        mask_copy(True).start()

    @pl.when(inner_low)
    def _():
        mask_copy(False).start()

    for sem, ref, base in ((0, fp, EDGE), (2, lp, EDGE)):
        pltpu.make_async_copy(ref.at[pl.ds(base, ROWS)], ref.at[pl.ds(base, ROWS)], in_sem.at[sem]).wait()

    @pl.when(inner_high)
    def _():
        for copy in halo_copies(True):
            copy.start()

    for sem, ref, base in ((1, fm, 0), (3, lm, 0)):
        pltpu.make_async_copy(ref.at[pl.ds(base, ROWS)], ref.at[pl.ds(base, ROWS)], in_sem.at[sem]).wait()

    @pl.when(inner_low)
    def _():
        for copy in halo_copies(False):
            copy.start()

    @pl.when(inner_low)
    def _():
        mask_copy(True).wait_recv()

    @pl.when(jnp.logical_not(inner_low))
    def _():
        mh[0] = jnp.zeros((8, LON), jnp.int32)
        fp[pl.ds(HALO, HALO)] = jnp.zeros((HALO, 16, LON), F32)
        lp[pl.ds(HALO, HALO)] = jnp.zeros((HALO, 8, 128), F32)

    @pl.when(inner_high)
    def _():
        mask_copy(False).wait_recv()

    @pl.when(jnp.logical_not(inner_high))
    def _():
        mh[1] = jnp.zeros((8, LON), jnp.int32)
        fm[pl.ds(ROWS, HALO)] = jnp.zeros((HALO, 16, LON), F32)
        lm[pl.ds(ROWS, HALO)] = jnp.zeros((HALO, 8, 128), F32)

    for ref, at in ((fp, 0), (fm, SIDE - HALO)):
        ref[pl.ds(at, HALO)] = jnp.zeros((HALO, 16, LON), F32)
    for ref, at in ((lp, 0), (lm, SIDE - HALO)):
        ref[pl.ds(at, HALO)] = jnp.zeros((HALO, 8, 128), F32)
    whole = jnp.concatenate([mh[0], mask[...], mh[1]], axis=0).astype(F32)
    column = lax.broadcasted_iota(jnp.int32, (112, LON), 1)
    for ref, value in (
        (msk, whole),
        (ox, jnp.where(column < LON - 1, whole * pltpu.roll(whole, LON - 1, 1), 0.0)),
        (oxm, jnp.where(column > 0, whole * pltpu.roll(whole, 1, 1), 0.0)),
        (oy, whole * pltpu.roll(whole, 111, 0)),
        (oym, whole * pltpu.roll(whole, 1, 0)),
    ):
        ref[...] = value.reshape(14, 8, LON)
    for ct in range(4):
        cols = pl.ds(128 * ct, 128)
        for i in range(2):
            place = 2 * ct + i
            for src, dst in (
                (oxm if i else ox, oxl.at[0]), (ox if i else oxm, oxl.at[1]),
                (oy, oyl.at[0]), (oym, oyl.at[1]), (msk, ml),
            ):
                pltpu.make_async_copy(src.at[:, :, cols], dst.at[:, :, place, :], lmask_sem.at[0]).start()
    for ref in (oxl, oyl, ml):
        pltpu.make_async_copy(ref, ref, lmask_sem.at[0]).wait()

    @pl.when(inner_low)
    def _():
        for copy in halo_copies(True):
            copy.wait_recv()

    @pl.when(inner_high)
    def _():
        for copy in halo_copies(False):
            copy.wait_recv()

    @pl.when(inner_high)
    def _():
        mask_copy(True).wait_send()
        for copy in halo_copies(True):
            copy.wait_send()

    @pl.when(inner_low)
    def _():
        mask_copy(False).wait_send()
        for copy in halo_copies(False):
            copy.wait_send()

    lane = lax.broadcasted_iota(jnp.int32, (8, 128), 1)
    odd = lax.rem(lax.broadcasted_iota(jnp.int32, (8, 128), 0), 2) == 1

    def wide(v):
        return jnp.concatenate([v] * 4, axis=1)

    def propagate(field, left, side, substep):
        a = scal[substep]
        coef = [
            (wide(a * table[0, pl.ds(16 * side + 8 * g, 8), :]), wide(a * table[1, pl.ds(16 * side + 8 * g, 8), :]))
            for g in range(2)
        ]
        coef_l = (a * table[0, pl.ds(32 + 8 * side, 8), :], a * table[1, pl.ds(32 + 8 * side, 8), :])
        open_y = oy if side == 0 else oym

        def block(b, carry):
            flows = list(carry)
            for step in range(BLOCK):
                j = step if side == 0 else BLOCK - 1 - step
                block_at = b if side == 0 else SIDE // BLOCK - 1 - b
                i = block_at * BLOCK + j
                e = (block_at + side, j)
                row = (block_at + side, slice(j, j + 1), slice(None))
                oy_row = open_y[row]
                for g in range(2):
                    right = g == side
                    x = field[i, pl.ds(8 * g, 8), :]
                    if substep == 0:
                        x = x * msk[row]
                    o = x * coef[g][0] * (ox if right else oxm)[row]
                    p = x * coef[g][1] * oy_row
                    inflow = pltpu.roll(o, 1 if right else LON - 1, 1)
                    field[i, pl.ds(8 * g, 8), :] = x - o + inflow - p + flows[g]
                    flows[g] = p
                x = left[i]
                if substep == 0:
                    x = x * ml[e]
                o = x * coef_l[0] * oxl[(side, *e)]
                p = x * coef_l[1] * oyl[(side, *e)]
                up = pltpu.roll(o, 1, 1)
                up = jnp.where(lane == 0, pltpu.roll(up, 2, 0), up)
                down = pltpu.roll(o, 127, 1)
                down = jnp.where(lane == 127, pltpu.roll(down, 6, 0), down)
                inflow = jnp.where(odd, down, up) if side == 0 else jnp.where(odd, up, down)
                left[i] = x - o + inflow - p + flows[2]
                flows[2] = p
            return tuple(flows)

        zero = jnp.zeros((8, LON), F32)
        lax.fori_loop(0, SIDE // BLOCK, block, (zero, zero, jnp.zeros((8, 128), F32)))

    for substep in range(NSUB):
        for side in range(2):
            propagate((fp, fm)[side], (lp, lm)[side], side, substep)

    def points(q):
        def row(j, _):
            r = q * GROUPS + j
            for ct in range(4):
                cols = pl.ds(128 * ct, 128)
                pb[r, pl.ds(MAIN * ct, 16), :] = fp[r + EDGE, :, cols].astype(BF16)
                pb[r, pl.ds(MAIN * ct + 16, 16), :] = fm[r, :, cols].astype(BF16)
            pb[r, pl.ds(4 * MAIN, 16), :] = jnp.concatenate([lp[r + EDGE], lm[r]], axis=0).astype(BF16)
            return 0

        lax.fori_loop(0, GROUPS, row, 0)

    def send_copy(q, partner):
        return pltpu.make_async_remote_copy(
            pb.at[q * GROUPS + partner], rm.at[q, me], send_sem.at[q], recv_sem.at[q],
            device_id=(partner, lat), device_id_type=MESH,
        )

    def back_copy(q, partner):
        return pltpu.make_async_remote_copy(
            ib.at[q, partner], ri.at[q * GROUPS + me], back_send.at[q], back_recv.at[q],
            device_id=(partner, lat), device_id_type=MESH,
        )

    for q in range(CHUNKS):
        points(q)
        for partner in partners:
            send_copy(q, partner).start()
        pltpu.make_async_copy(pb.at[q * GROUPS + me], rm.at[q, me], recv_sem.at[q]).start()

    for copy in w_copies:
        copy.wait()

    def select_columns(i, _):
        rows = pl.ds(pl.multiple_of(i * 384, 384), 384)
        wi[rows, :] = jnp.dot(win[rows, :], perm[...], preferred_element_type=F32).astype(BF16)
        return 0

    def select_rows(i, _):
        rows = pl.ds(pl.multiple_of(i * 384, 384), 384)
        wo[rows, pl.ds(0, K)] = jnp.dot(perm[rows, :], wout[...], preferred_element_type=F32).astype(BF16)
        return 0

    def build(across):
        def tile(i, _):
            start = pl.multiple_of(i * 128, 128)
            rows = start + lax.broadcasted_iota(jnp.int32, (128, K), 0)
            cols = lax.broadcasted_iota(jnp.int32, (128, K), 1)
            hit = natural(cols) == rows if across else natural(rows) == cols
            perm[pl.ds(start, 128), :] = jnp.where(hit, 1.0, 0.0).astype(BF16)
            return 0

        lax.fori_loop(0, K // 128, tile, 0)

    build(True)
    lax.fori_loop(0, 3, select_columns, 0)
    wi[pl.ds(K, HID - K), :] = mean_w[...]
    build(False)
    lax.fori_loop(0, 3, select_rows, 0)
    wo[:, pl.ds(K, HID - K)] = jnp.zeros((K, HID - K), BF16)

    def sources(q):
        lf[...] = rm[q, :, pl.ds(4 * MAIN, 16), :].reshape(16 * GROUPS, 128).astype(F32)
        for ct in range(4):
            for i in range(2):
                rl[pl.ds(64 * i, 64), pl.ds(128 * ct, 128)] = lf[pl.ds(2 * ct + i, 64, stride=8), :].astype(BF16)

        def right_side():
            main = [rm[q, :, pl.ds(MAIN * ct, MAIN), :].reshape(MAIN * GROUPS, 128) for ct in range(4)]
            return jnp.concatenate([jnp.concatenate(main, axis=1), rl[...]], axis=0)

        for part in range(2):
            hidden = jnp.dot(wi[pl.ds(TILE1 * part, TILE1), :], right_side(), preferred_element_type=F32)
            sq[pl.ds(TILE1 * part, TILE1), :] = (hidden * hidden).astype(BF16)
            if part == 1:
                energy = hidden[K - TILE1 : K - TILE1 + 1] + hidden[K - TILE1 + 1 : K - TILE1 + 2]
                hq[...] = jnp.broadcast_to(energy / (1.0 + energy), (8, LON))
        square = sq[...]

        def rows_of(i, _):
            base = pl.multiple_of(i * TILE2, TILE2)
            dests = TILE2 // MAIN
            transfer = jnp.dot(wo[pl.ds(base, TILE2), :], square, preferred_element_type=F32)
            for ct in range(4):
                where = (q, pl.ds(i * dests, dests), pl.ds(MAIN * ct, MAIN), slice(None))
                energy = rm[where].astype(F32).reshape(TILE2, 128)
                rate = gain[pl.ds(base, TILE2), :] - damp[pl.ds(base, TILE2), :] * hq[0:1, 128 * ct : 128 * ct + 128]
                result = energy * rate + 0.125 * transfer[:, 128 * ct : 128 * ct + 128]
                ib[where] = result.astype(BF16).reshape(dests, MAIN, 128)
            return 0

        lax.fori_loop(0, MAIN * GROUPS // TILE2, rows_of, 0)
        transfer = jnp.dot(wo[pl.ds(1024, 128), :], square, preferred_element_type=F32)
        for ct in range(4):
            cols = slice(128 * ct, 128 * ct + 128)
            rate = gain[pl.ds(1024, 128), :] - damp[pl.ds(1024, 128), :] * hq[0:1, cols]
            result = rl[:, cols].astype(F32) * rate + 0.125 * transfer[:, cols]
            for i in range(2):
                tl[pl.ds(2 * ct + i, 64, stride=8), :] = result[64 * i : 64 * i + 64]
        ib[q, :, pl.ds(4 * MAIN, 16), :] = tl[...].astype(BF16).reshape(GROUPS, 16, 128)

    def chunk(q, _):
        pltpu.make_async_copy(rm.at[q], rm.at[q], recv_sem.at[q]).wait()
        sources(q)
        for partner in partners:
            back_copy(q, partner).start()
        pltpu.make_async_copy(ib.at[q, me], ri.at[q * GROUPS + me], back_recv.at[q]).start()
        return 0

    lax.fori_loop(0, CHUNKS, chunk, 0)

    def store_copies(q):
        first = q * GROUPS
        copies = []
        for quadrant in range(4):
            src, base = (fp, EDGE) if quadrant < 2 else (fm, 0)
            for t in range(8):
                copies.append(
                    pltpu.make_async_copy(
                        src.at[pl.ds(base + first, GROUPS), 8 * (quadrant % 2) + t, :],
                        out.at[0, direction(quadrant, t), pl.ds(first, GROUPS), :],
                        out_sem.at[0],
                    )
                )
            src = lp if quadrant < 2 else lm
            for ct in range(4):
                copies.append(
                    pltpu.make_async_copy(
                        src.at[pl.ds(base + first, GROUPS), 2 * ct + quadrant % 2, :],
                        out.at[0, direction(quadrant, 8), pl.ds(first, GROUPS), pl.ds(128 * ct, 128)],
                        out_sem.at[0],
                    )
                )
        return copies

    for q in range(CHUNKS):
        pltpu.make_async_copy(
            ri.at[pl.ds(q * GROUPS, GROUPS)], ri.at[pl.ds(q * GROUPS, GROUPS)], back_recv.at[q]
        ).wait()

        def rows(b, _):
            block_at = q * (GROUPS // BLOCK) + b
            for j in range(BLOCK):
                r = block_at * BLOCK + j
                for ct in range(4):
                    cols = pl.ds(128 * ct, 128)
                    sea = msk[block_at + 1, j : j + 1, cols]
                    fp[r + EDGE, :, cols] += ri[r, pl.ds(MAIN * ct, 16), :].astype(F32) * sea
                    fm[r, :, cols] += ri[r, pl.ds(MAIN * ct + 16, 16), :].astype(F32) * sea
                left = ri[r, pl.ds(4 * MAIN, 16), :].astype(F32)
                lp[r + EDGE] += left[0:8] * ml[block_at + 1, j]
                lm[r] += left[8:16] * ml[block_at + 1, j]
            return 0

        lax.fori_loop(0, GROUPS // BLOCK, rows, 0)
        for copy in store_copies(q):
            copy.start()

    sent = pb.at[pl.ds(0, len(ORDER))]
    for q in range(CHUNKS):
        pltpu.make_async_copy(sent, sent, send_sem.at[q]).wait()
        pltpu.make_async_copy(sent, sent, back_send.at[q]).wait()
    for ref in (fp.at[pl.ds(EDGE, ROWS)], fm.at[pl.ds(0, ROWS)], lp.at[pl.ds(EDGE, ROWS)], lm.at[pl.ds(0, ROWS)]):
        pltpu.make_async_copy(ref, ref, out_sem.at[0]).wait()


def ordered(values):
    parts = values.reshape(NFREQ, 4, 9)
    main = parts[:, :, :8].reshape(-1)
    left = jnp.transpose(parts[:, :, 8].reshape(NFREQ, 2, 2), (2, 0, 1)).reshape(-1)
    return jnp.concatenate([main, left])


def local(spectrum, sea_mask, point_index, band_counts, sub_counts, mix_in, mix_out, growth, damping):
    freq = lax.axis_index("comp").astype(F32)
    steps = sub_counts[0]
    speed = 1.4 * jnp.power(jnp.float32(0.93), freq)
    active = (steps > jnp.arange(NSUB)).astype(F32)
    scal = speed * active / steps.astype(F32)
    raw = np.power(np.float64(1.1), np.arange(NFREQ))
    weight = np.repeat(raw / (NDIR * raw.sum()), NDIR).astype(np.float32)
    nat = np.asarray(natural_np())
    weight = weight[nat]
    high = weight.astype(jnp.bfloat16)
    low = (weight - high.astype(np.float32)).astype(jnp.bfloat16)
    mean_w = np.zeros((HID - K, K), jnp.bfloat16)
    mean_w[0], mean_w[1] = high, low
    gain = jnp.broadcast_to(0.5 * ordered(growth)[:, None], (K, 128))
    damp = jnp.broadcast_to(0.5 * ordered(damping)[:, None], (K, 128))
    hbm, vmem = pl.BlockSpec(memory_space=pl.ANY), pl.BlockSpec(memory_space=pltpu.VMEM)
    smem = pl.BlockSpec(memory_space=pltpu.SMEM)
    dma, VM = pltpu.SemaphoreType.DMA, pltpu.VMEM
    return pl.pallas_call(
        kernel,
        name="wave_step",
        out_shape=jax.ShapeDtypeStruct(spectrum.shape, F32),
        in_specs=[hbm, vmem, smem, vmem, hbm, hbm, vmem, vmem, vmem],
        out_specs=hbm,
        scratch_shapes=[
            VM((SIDE, 16, LON), F32), VM((SIDE, 16, LON), F32), VM((SIDE, 8, 128), F32), VM((SIDE, 8, 128), F32),
            VM((14, 8, LON), F32), VM((2, 8, LON), jnp.int32),
            VM((14, 8, LON), F32), VM((14, 8, LON), F32), VM((14, 8, LON), F32), VM((14, 8, LON), F32),
            VM((2, 14, 8, 8, 128), F32), VM((2, 14, 8, 8, 128), F32), VM((14, 8, 8, 128), F32),
            VM((ROWS, MSG, 128), BF16), VM((CHUNKS, GROUPS, MSG, 128), BF16),
            VM((CHUNKS, GROUPS, MSG, 128), BF16), VM((ROWS, MSG, 128), BF16),
            VM((K, K), BF16), VM((K, K), BF16), VM((K, K), BF16), VM((HID, K), BF16), VM((K, HID), BF16),
            VM((HID, LON), BF16), VM((8, LON), F32), VM((16 * GROUPS, 128), F32), VM((128, LON), BF16),
            VM((16 * GROUPS, 128), F32),
            dma((4,)), dma((2, 2)), dma((2, 2)), dma((2,)), dma((2,)), dma((1,)), dma((2,)), dma((1,)),
            dma((CHUNKS,)), dma((CHUNKS,)), dma((CHUNKS,)), dma((CHUNKS,)), dma((1,)),
        ],
        compiler_params=pltpu.CompilerParams(
            collective_id=0, has_side_effects=True, vmem_limit_bytes=60 * 1024 * 1024
        ),
    )(spectrum, sea_mask, scal, jnp.asarray(angle_tables()), mix_in, mix_out, jnp.asarray(mean_w), gain, damp)


def natural_np():
    c = np.arange(K)
    k = c & 31
    main = 36 * (c >> 5) + 9 * (k >> 3) + (k & 7)
    r = c - 1024
    left = 36 * ((r & 63) >> 1) + 9 * (2 * (r & 1) + (r >> 6)) + 8
    return np.where(c < 1024, main, left)


def solution(mesh):
    return jax.shard_map(
        local,
        mesh=mesh,
        in_specs=(
            P("comp", None, "lat", None),
            P("lat", None),
            P("lat", None),
            P("lat"),
            P("comp"),
            P(),
            P(),
            P(),
            P(),
        ),
        out_specs=P("comp", None, "lat", None),
        check_vma=False,
    )
```

profile of v0, /device:TPU:1, one launch (start us, length us, event | category | flops | bytes accessed | tf_op | source)
XLA Modules:
  0.0 127.1 jit_solution(15495189223024676473)
XLA Ops:
  0.7 0.6 fusion.scal
  1.3 0.8 copy.14
  2.1 0.8 copy.17
  2.9 0.1 copy.19
  3.0 0.1 concatenate.26
  3.2 0.1 copy.16
  3.2 0.1 concatenate.23
  3.4 0.1 copy.18
  3.5 0.1 concatenate.25
  3.6 0.1 copy.15
  3.7 0.1 concatenate.22
  3.8 1.0 broadcast_in_dim.4.gain
  4.9 1.0 broadcast_in_dim.5.damp
  5.9 113.8 %wave_step.1 = f32[1,36,96,512]{3,2,1,0:T(8,128)} custom-call(f32[1,36,96,512]{3,2,1,0:T(8,128)} %spec.1, s32[96,512]{1,0:T(8,128)} %mask.1, f32[4]{0:T(128)} %fusion.scal, f32[2,48,128]{2,1,0:T(8,128)} %constant.18.clone.table, bf16[1152,1152]{1,0:T(8,128)(2,1)} %w_in.1, bf16[1152,1152]{1,0:T(8,128)(2,1)} %w_out.1, bf16[32,1152]{1,0:T(8,128)(2,1)} %constant.19.clone.mean_w, ...), custom_call_target="tpu_custom_call" | custom-call | tf_op jit(solution)/shard_map/wave_step/pallas_call | solution.py:467
  119.8 7.3 %copy.22 = f32[1,36,96,512]{3,2,1,0:T(8,128)} copy(f32[1,36,96,512]{3,2,1,0:T(8,128)} %wave_step.1) | data formatting | bytes 14155776
  (8 shorter events, 0.0 us)
where the time goes:
time: 127 us
  Pallas kernels  114 us (90%)
  local copies, waits for them, and re-layouts  11.9 us (9%)
    pallas_call x1, Pallas kernels, local(): pl.pallas_call(kernel, name='wave_step', out_shape=jax.ShapeDtypeStruct(s...  114 us
    unnamed x3, local copies, waits for them, and re-layouts  8.93 us

commit v1 on v0

v1 whole, which is shorter than its diff:
```python
import functools
import math

import jax
import jax.numpy as jnp
import numpy as np
from jax import lax
from jax.experimental import pallas as pl
from jax.experimental.pallas import tpu as pltpu
from jax.sharding import PartitionSpec as P

MESH = pl.DeviceIdType.MESH
F32, BF16 = jnp.float32, jnp.bfloat16
NSUB = 4
NDIR, NFREQ, ROWS, LON = 36, 32, 96, 512
K = NDIR * NFREQ
GROUPS = 32
CHUNKS = ROWS // GROUPS
HALO = 4
EDGE = 8
SIDE = ROWS + 2 * EDGE
PHASES = (1, 2, 0)
MAIN = 32
MSG = 4 * MAIN + 16
HID = 1184
TILE1 = HID // 2
TILE2 = 512
BLOCK = 8

LATIN = [((i + dy) % 4, dy) for i in range(4) for dy in (1, 3, 2, 0) if ((i + dy) % 4, dy) != (0, 0)]
ORDER = [(dz, dy, dc) for dz, dy in LATIN for dc in (0, 1)] + [(0, 0, 1)]


def direction(quadrant, place):
    return 9 * quadrant + place


def angle_tables():
    main = [direction(q, t) for q in range(4) for t in range(8)]
    left_plus = [direction(i, 8) for _ in range(4) for i in range(2)]
    left_minus = [direction(2 + i, 8) for _ in range(4) for i in range(2)]
    angles = (np.array(main + left_plus + left_minus, np.float32) + np.float32(0.5)) * np.float32(2.0 * np.pi / NDIR)
    table = np.stack([np.abs(np.cos(angles)), np.abs(np.sin(angles))]).astype(np.float32)
    return np.ascontiguousarray(np.broadcast_to(table[:, :, None], (2, 48, 128)))


def component(c, where=jnp.where):
    k, r = c & 31, c - 1024
    left = c >= 1024
    freq = where(left, (r & 63) >> 1, c >> 5)
    turn = where(left, 9 * (2 * (r & 1) + (r >> 6)) + 8, 9 * (k >> 3) + (k & 7))
    return freq, turn


def natural(c, where=jnp.where):
    freq, turn = component(c, where)
    return NDIR * freq + turn


def first_row(side, q):
    return EDGE + q * GROUPS + (EDGE if q else 0) if side == 0 else q * GROUPS + (EDGE if q == 2 else 0)


def kernel(
    spec, mask, counts, speed, table, w_in, w_out, mean_w, growth, damping,
    out,
    fp, fm, lp, lm, mk, tb, msk, mh, ox, oxm, oy, oym, oxl, oyl, ml, flow, flow_l,
    pb, rm, ib, ri, win, wout, perm, wi, wo, gr, dp, gain, damp, sq, hq, lf, rl, tl,
    in_sem, small_sem, halo_send, halo_recv, mask_send, mask_recv, w_sem,
    send_sem, recv_sem, back_send, back_recv, out_sem,
):
    me, lat = lax.axis_index("comp"), lax.axis_index("lat")
    z, y, core = lax.div(me, 8), lax.rem(lax.div(me, 2), 4), lax.rem(me, 2)
    partners = [
        (lax.rem(z + dz, 4) * 4 + lax.rem(y + dy, 4)) * 2 + lax.rem(core + dc, 2) for dz, dy, dc in ORDER
    ]
    fields, lefts = (fp, fm), (lp, lm)

    small = [
        pltpu.make_async_copy(src, dst, small_sem.at[i])
        for i, (src, dst) in enumerate(((mask, mk), (table, tb), (growth, gr), (damping, dp)))
    ]
    small[0].start()
    small[1].start()

    spans = {1: ((24, 40), (32, 40)), 2: ((64, 32), (64, 32)), 0: ((0, 32), (0, 32))}

    def landing(side, q):
        row, rows = spans[q][side]
        return row, pl.ds(first_row(side, q) - (EDGE if q == 1 and side == 0 else 0), rows), rows

    def load(q):
        for quadrant in range(4):
            side, i = divmod(quadrant, 2)
            row, there, rows = landing(side, q)
            for t in range(8):
                pltpu.make_async_copy(
                    spec.at[0, direction(quadrant, t), pl.ds(row, rows)], fields[side].at[there, 8 * i + t, :],
                    in_sem.at[q, side],
                ).start()
            for ct in range(4):
                pltpu.make_async_copy(
                    spec.at[0, direction(quadrant, 8), pl.ds(row, rows), pl.ds(128 * ct, 128)],
                    lefts[side].at[there, 2 * ct + i, :],
                    in_sem.at[q, 2 + side],
                ).start()

    def loaded(q):
        for side in range(2):
            _, there, _ = landing(side, q)
            for ref, sem in ((fields[side], side), (lefts[side], 2 + side)):
                pltpu.make_async_copy(ref.at[there], ref.at[there], in_sem.at[q, sem]).wait()

    load(1)

    barrier = pltpu.get_barrier_semaphore()
    for partner in partners:
        pl.semaphore_signal(barrier, inc=1, device_id=(partner, lat), device_id_type=MESH)
    inner_low, inner_high = lat > 0, lat < 3

    @pl.when(inner_low)
    def _():
        pl.semaphore_signal(barrier, inc=1, device_id=(me, lat - 1), device_id_type=MESH)

    @pl.when(inner_high)
    def _():
        pl.semaphore_signal(barrier, inc=1, device_id=(me, lat + 1), device_id_type=MESH)

    load(2)
    load(0)
    w_copies = [
        pltpu.make_async_copy(w_in, win, w_sem.at[0]),
        pltpu.make_async_copy(w_out, wout, w_sem.at[1]),
        pltpu.make_async_copy(mean_w, wi.at[pl.ds(K, HID - K)], w_sem.at[2]),
    ]
    for copy in w_copies:
        copy.start()
    small[2].start()
    small[3].start()

    lane = lax.broadcasted_iota(jnp.int32, (8, 128), 1)
    sub = lax.broadcasted_iota(jnp.int32, (8, 128), 0)
    odd = lax.rem(sub, 2) == 1
    wide_sub = lax.broadcasted_iota(jnp.int32, (8, LON), 0)
    wide_lane = lax.broadcasted_iota(jnp.int32, (8, LON), 1)

    def open_lon(b):
        here = msk[b]
        ox[b] = jnp.where(wide_lane < LON - 1, here * pltpu.roll(here, LON - 1, 1), 0.0)
        oxm[b] = jnp.where(wide_lane > 0, here * pltpu.roll(here, 1, 1), 0.0)

    def open_up(b):
        oy[b] = msk[b] * jnp.where(wide_sub == 7, pltpu.roll(msk[b + 1], 7, 0), pltpu.roll(msk[b], 7, 0))

    def open_down(b):
        oym[b] = msk[b] * jnp.where(wide_sub == 0, pltpu.roll(msk[b - 1], 1, 0), pltpu.roll(msk[b], 1, 0))

    def stacked(ref, b, j):
        part = [ref[b, j : j + 1, 128 * ct : 128 * ct + 128] for ct in range(4)]
        return jnp.where(sub < 4, jnp.where(sub < 2, part[0], part[1]), jnp.where(sub < 6, part[2], part[3]))

    def left_lon(b):
        for j in range(BLOCK):
            right, leftward = stacked(ox, b, j), stacked(oxm, b, j)
            oxl[0, b, j] = jnp.where(odd, leftward, right)
            oxl[1, b, j] = jnp.where(odd, right, leftward)
            ml[b, j] = stacked(msk, b, j)

    def left_up(b):
        for j in range(BLOCK):
            oyl[0, b, j] = stacked(oy, b, j)

    def left_down(b):
        for j in range(BLOCK):
            oyl[1, b, j] = stacked(oym, b, j)

    small[0].wait()
    msk[pl.ds(1, 12)] = mk[...].astype(F32).reshape(12, 8, LON)

    def inner_openings(b, _):
        open_lon(b)
        open_up(b)
        open_down(b)
        left_lon(b)
        left_up(b)
        left_down(b)
        return 0

    lax.fori_loop(2, 12, inner_openings, 0)
    small[1].wait()
    steps = jnp.full((8, 128), counts[0], jnp.int32)
    rate = jnp.full((8, 128), speed[me], F32) / steps.astype(F32)

    flow[0] = jnp.zeros((2, NSUB, 16, LON), F32)
    flow_l[0] = jnp.zeros((2, NSUB, 8, 128), F32)

    def wide(v):
        return jnp.concatenate([v] * 4, axis=1)

    def propagate(q, side, substep):
        field, left = fields[side], lefts[side]
        a = jnp.where(steps > substep, rate, 0.0)
        coef = [
            (wide(a * tb[0, pl.ds(16 * side + 8 * g, 8), :]), wide(a * tb[1, pl.ds(16 * side + 8 * g, 8), :]))
            for g in range(2)
        ]
        coef_l = (a * tb[0, pl.ds(32 + 8 * side, 8), :], a * tb[1, pl.ds(32 + 8 * side, 8), :])
        open_y = oym if side else oy
        run_up = q == 1 or q == 2 * side
        first = first_row(side, q) // BLOCK
        low = first - (1 if run_up and side == 0 else 0)
        high = first + GROUPS // BLOCK + (1 if run_up and side == 1 else 0)
        if side == 0:
            ahead = 0 if q == 0 else -1
        else:
            ahead = 0 if q == 2 else 1

        def block(n, carry):
            flows = list(carry)
            b = high - 1 - n if side else low + n
            for step in range(BLOCK):
                j = BLOCK - 1 - step if side else step
                i = b * BLOCK + j
                e = (b + ahead, j)
                row = (b + ahead, slice(j, j + 1), slice(None))
                oy_row = open_y[row]
                for g in range(2):
                    right = g == side
                    x = field[i, pl.ds(8 * g, 8), :]
                    if substep == 0:
                        x = x * msk[row]
                    o = x * coef[g][0] * (ox if right else oxm)[row]
                    p = x * coef[g][1] * oy_row
                    inflow = pltpu.roll(o, 1 if right else LON - 1, 1)
                    field[i, pl.ds(8 * g, 8), :] = x - o + inflow - p + flows[g]
                    flows[g] = p
                x = left[i]
                if substep == 0:
                    x = x * ml[e]
                o = x * coef_l[0] * oxl[(side, *e)]
                p = x * coef_l[1] * oyl[(side, *e)]
                up = pltpu.roll(o, 1, 1)
                up = jnp.where(lane == 0, pltpu.roll(up, 2, 0), up)
                down = pltpu.roll(o, 127, 1)
                down = jnp.where(lane == 127, pltpu.roll(down, 6, 0), down)
                inflow = jnp.where(odd, down, up) if side == 0 else jnp.where(odd, up, down)
                left[i] = x - o + inflow - p + flows[2]
                flows[2] = p
            return tuple(flows)

        slot = 0 if run_up else 1
        start = (flow[slot, side, substep, 0:8], flow[slot, side, substep, 8:16], flow_l[slot, side, substep])
        end = lax.fori_loop(0, high - low, block, start)
        if q == 1:
            flow[1, side, substep, 0:8] = end[0]
            flow[1, side, substep, 8:16] = end[1]
            flow_l[1, side, substep] = end[2]

    def passes(q):
        for substep in range(NSUB):
            for side in range(2):
                propagate(q, side, substep)

    def mask_copy(up):
        return pltpu.make_async_remote_copy(
            mk.at[pl.ds(88, 8)] if up else mk.at[pl.ds(0, 8)],
            mh.at[0 if up else 1],
            mask_send.at[0 if up else 1],
            mask_recv.at[0 if up else 1],
            device_id=(me, lat + 1 if up else lat - 1),
            device_id_type=MESH,
        )

    def halo_copies(up):
        side = 0 if up else 1
        src, dst = (SIDE - HALO, EDGE - HALO) if up else (0, SIDE - EDGE)
        return [
            pltpu.make_async_remote_copy(
                ref.at[pl.ds(src, HALO)], ref.at[pl.ds(dst, HALO)], halo_send.at[side, i], halo_recv.at[side, i],
                device_id=(me, lat + 1 if up else lat - 1), device_id_type=MESH,
            )
            for i, ref in enumerate((fields[side], lefts[side]))
        ]

    def edge_copies(up):
        return [mask_copy(up), *halo_copies(up)]

    for side, at in ((0, 0), (1, SIDE - HALO)):
        fields[side][pl.ds(at, HALO)] = jnp.zeros((HALO, 16, LON), F32)
        lefts[side][pl.ds(at, HALO)] = jnp.zeros((HALO, 8, 128), F32)

    loaded(1)
    passes(1)
    neighbours = jnp.where(inner_low, 1, 0) + jnp.where(inner_high, 1, 0)
    pl.semaphore_wait(barrier, len(ORDER) + neighbours)
    loaded(2)
    loaded(0)

    @pl.when(inner_high)
    def _():
        for copy in edge_copies(True):
            copy.start()

    @pl.when(inner_low)
    def _():
        for copy in edge_copies(False):
            copy.start()

    def points(q):
        low, high = first_row(0, q), first_row(1, q)

        def row(j, _):
            r = q * GROUPS + j
            for ct in range(4):
                cols = pl.ds(128 * ct, 128)
                pb[r, pl.ds(MAIN * ct, 16), :] = fp[low + j, :, cols].astype(BF16)
                pb[r, pl.ds(MAIN * ct + 16, 16), :] = fm[high + j, :, cols].astype(BF16)
            pb[r, pl.ds(4 * MAIN, 16), :] = jnp.concatenate([lp[low + j], lm[high + j]], axis=0).astype(BF16)
            return 0

        lax.fori_loop(0, GROUPS, row, 0)

    def send_copy(q, partner):
        return pltpu.make_async_remote_copy(
            pb.at[q * GROUPS + partner], rm.at[q, me], send_sem.at[q], recv_sem.at[q],
            device_id=(partner, lat), device_id_type=MESH,
        )

    def back_copy(q, partner):
        return pltpu.make_async_remote_copy(
            ib.at[q, partner], ri.at[q * GROUPS + me], back_send.at[q], back_recv.at[q],
            device_id=(partner, lat), device_id_type=MESH,
        )

    def send(q):
        points(q)
        for partner in partners:
            send_copy(q, partner).start()
        pltpu.make_async_copy(pb.at[q * GROUPS + me], rm.at[q, me], recv_sem.at[q]).start()

    send(1)

    def select_columns(i, _):
        rows = pl.ds(pl.multiple_of(i * 384, 384), 384)
        wi[rows, :] = jnp.dot(win[rows, :], perm[...], preferred_element_type=F32).astype(BF16)
        return 0

    def select_rows(i, _):
        rows = pl.ds(pl.multiple_of(i * 384, 384), 384)
        wo[rows, pl.ds(0, K)] = jnp.dot(perm[rows, :], wout[...], preferred_element_type=F32).astype(BF16)
        return 0

    def build(across):
        def tile(i, _):
            start = pl.multiple_of(i * 128, 128)
            rows = start + lax.broadcasted_iota(jnp.int32, (128, K), 0)
            cols = lax.broadcasted_iota(jnp.int32, (128, K), 1)
            hit = natural(cols) == rows if across else natural(rows) == cols
            perm[pl.ds(start, 128), :] = jnp.where(hit, 1.0, 0.0).astype(BF16)
            return 0

        lax.fori_loop(0, K // 128, tile, 0)

    for copy in w_copies:
        copy.wait()
    build(True)
    lax.fori_loop(0, 3, select_columns, 0)

    @pl.when(inner_low)
    def _():
        for copy in edge_copies(True):
            copy.wait_recv()

    @pl.when(inner_high)
    def _():
        for copy in edge_copies(False):
            copy.wait_recv()

    @pl.when(inner_high)
    def _():
        for copy in edge_copies(True):
            copy.wait_send()

    @pl.when(inner_low)
    def _():
        for copy in edge_copies(False):
            copy.wait_send()

    @pl.when(jnp.logical_not(inner_low))
    def _():
        mh[0] = jnp.zeros((8, LON), jnp.int32)
        fp[pl.ds(HALO, HALO)] = jnp.zeros((HALO, 16, LON), F32)
        lp[pl.ds(HALO, HALO)] = jnp.zeros((HALO, 8, 128), F32)

    @pl.when(jnp.logical_not(inner_high))
    def _():
        mh[1] = jnp.zeros((8, LON), jnp.int32)
        fm[pl.ds(SIDE - EDGE, HALO)] = jnp.zeros((HALO, 16, LON), F32)
        lm[pl.ds(SIDE - EDGE, HALO)] = jnp.zeros((HALO, 8, 128), F32)

    msk[0] = mh[0].astype(F32)
    msk[13] = mh[1].astype(F32)
    for b in (0, 1, 12, 13):
        open_lon(b)
        left_lon(b)
    for b in (0, 1, 12):
        open_up(b)
        left_up(b)
    for b in (1, 12, 13):
        open_down(b)
        left_down(b)

    for q in PHASES[1:]:
        passes(q)
        send(q)

    build(False)
    lax.fori_loop(0, 3, select_rows, 0)
    wo[:, pl.ds(K, HID - K)] = jnp.zeros((K, HID - K), BF16)

    small[2].wait()
    small[3].wait()

    def rates(i, _):
        start = pl.multiple_of(i * 128, 128)
        place = start + lax.broadcasted_iota(jnp.int32, (128, NFREQ), 0)
        freq, _ = component(place)
        pick = jnp.where(freq == lax.broadcasted_iota(jnp.int32, (128, NFREQ), 1), 0.5, 0.0)
        _, turn = component(start + lax.broadcasted_iota(jnp.int32, (128, NDIR), 0))
        hit = turn == lax.broadcasted_iota(jnp.int32, (128, NDIR), 1)
        for src, dst in ((gr, gain), (dp, damp)):
            rows = jnp.dot(pick, src[...], preferred_element_type=F32, precision=lax.Precision.HIGHEST)
            picked = jnp.sum(jnp.where(hit, rows, 0.0), axis=1, keepdims=True)
            dst[pl.ds(start, 128), :] = jnp.broadcast_to(picked, (128, 128))
        return 0

    lax.fori_loop(0, K // 128, rates, 0)

    def sources(q):
        lf[...] = rm[q, :, pl.ds(4 * MAIN, 16), :].reshape(16 * GROUPS, 128).astype(F32)
        for ct in range(4):
            for i in range(2):
                rl[pl.ds(64 * i, 64), pl.ds(128 * ct, 128)] = lf[pl.ds(2 * ct + i, 64, stride=8), :].astype(BF16)

        def right_side():
            main = [rm[q, :, pl.ds(MAIN * ct, MAIN), :].reshape(MAIN * GROUPS, 128) for ct in range(4)]
            return jnp.concatenate([jnp.concatenate(main, axis=1), rl[...]], axis=0)

        for part in range(2):
            hidden = jnp.dot(wi[pl.ds(TILE1 * part, TILE1), :], right_side(), preferred_element_type=F32)
            sq[pl.ds(TILE1 * part, TILE1), :] = (hidden * hidden).astype(BF16)
            if part == 1:
                energy = hidden[K - TILE1 : K - TILE1 + 1] + hidden[K - TILE1 + 1 : K - TILE1 + 2]
                hq[...] = jnp.broadcast_to(energy / (1.0 + energy), (8, LON))
        square = sq[...]

        def rows_of(i, _):
            base = pl.multiple_of(i * TILE2, TILE2)
            dests = TILE2 // MAIN
            transfer = jnp.dot(wo[pl.ds(base, TILE2), :], square, preferred_element_type=F32)
            for ct in range(4):
                where = (q, pl.ds(i * dests, dests), pl.ds(MAIN * ct, MAIN), slice(None))
                energy = rm[where].astype(F32).reshape(TILE2, 128)
                rate = gain[pl.ds(base, TILE2), :] - damp[pl.ds(base, TILE2), :] * hq[0:1, 128 * ct : 128 * ct + 128]
                result = energy * rate + 0.125 * transfer[:, 128 * ct : 128 * ct + 128]
                ib[where] = result.astype(BF16).reshape(dests, MAIN, 128)
            return 0

        lax.fori_loop(0, MAIN * GROUPS // TILE2, rows_of, 0)
        transfer = jnp.dot(wo[pl.ds(1024, 128), :], square, preferred_element_type=F32)
        for ct in range(4):
            cols = slice(128 * ct, 128 * ct + 128)
            rate = gain[pl.ds(1024, 128), :] - damp[pl.ds(1024, 128), :] * hq[0:1, cols]
            result = rl[:, cols].astype(F32) * rate + 0.125 * transfer[:, cols]
            for i in range(2):
                tl[pl.ds(2 * ct + i, 64, stride=8), :] = result[64 * i : 64 * i + 64]
        ib[q, :, pl.ds(4 * MAIN, 16), :] = tl[...].astype(BF16).reshape(GROUPS, 16, 128)

    def chunk(q, _):
        pltpu.make_async_copy(rm.at[q], rm.at[q], recv_sem.at[q]).wait()
        sources(q)
        for partner in partners:
            back_copy(q, partner).start()
        pltpu.make_async_copy(ib.at[q, me], ri.at[q * GROUPS + me], back_recv.at[q]).start()
        return 0

    for q in PHASES:
        chunk(q, 0)

    def store_copies(q):
        first = q * GROUPS
        copies = []
        for quadrant in range(4):
            side = quadrant // 2
            src, here = fields[side], pl.ds(first_row(side, q), GROUPS)
            for t in range(8):
                copies.append(
                    pltpu.make_async_copy(
                        src.at[here, 8 * (quadrant % 2) + t, :],
                        out.at[0, direction(quadrant, t), pl.ds(first, GROUPS), :],
                        out_sem.at[0],
                    )
                )
            src = lefts[side]
            for ct in range(4):
                copies.append(
                    pltpu.make_async_copy(
                        src.at[here, 2 * ct + quadrant % 2, :],
                        out.at[0, direction(quadrant, 8), pl.ds(first, GROUPS), pl.ds(128 * ct, 128)],
                        out_sem.at[0],
                    )
                )
        return copies

    for q in PHASES:
        low, high = first_row(0, q), first_row(1, q)
        pltpu.make_async_copy(
            ri.at[pl.ds(q * GROUPS, GROUPS)], ri.at[pl.ds(q * GROUPS, GROUPS)], back_recv.at[q]
        ).wait()

        def rows(b, _):
            block_at = q * (GROUPS // BLOCK) + b + 1
            for j in range(BLOCK):
                here = b * BLOCK + j
                r = q * GROUPS + here
                for ct in range(4):
                    cols = pl.ds(128 * ct, 128)
                    sea = msk[block_at, j : j + 1, cols]
                    fp[low + here, :, cols] += ri[r, pl.ds(MAIN * ct, 16), :].astype(F32) * sea
                    fm[high + here, :, cols] += ri[r, pl.ds(MAIN * ct + 16, 16), :].astype(F32) * sea
                left = ri[r, pl.ds(4 * MAIN, 16), :].astype(F32)
                lp[low + here] += left[0:8] * ml[block_at, j]
                lm[high + here] += left[8:16] * ml[block_at, j]
            return 0

        lax.fori_loop(0, GROUPS // BLOCK, rows, 0)
        for copy in store_copies(q):
            copy.start()

    sent = pb.at[pl.ds(0, len(ORDER))]
    for q in range(CHUNKS):
        pltpu.make_async_copy(sent, sent, send_sem.at[q]).wait()
        pltpu.make_async_copy(sent, sent, back_send.at[q]).wait()
    for ref in (fp.at[pl.ds(0, ROWS)], fm.at[pl.ds(0, ROWS)], lp.at[pl.ds(0, ROWS)], lm.at[pl.ds(0, ROWS)]):
        pltpu.make_async_copy(ref, ref, out_sem.at[0]).wait()


def local(spectrum, sea_mask, point_index, band_counts, sub_counts, mix_in, mix_out, growth, damping):
    speed = (1.4 * np.power(np.float64(0.93), np.arange(NFREQ))).astype(np.float32)
    raw = np.power(np.float64(1.1), np.arange(NFREQ))
    weight = np.repeat(raw / (NDIR * raw.sum()), NDIR).astype(np.float32)
    weight = weight[natural(np.arange(K), np.where)]
    high = weight.astype(jnp.bfloat16)
    low = (weight - high.astype(np.float32)).astype(jnp.bfloat16)
    mean_w = np.zeros((HID - K, K), jnp.bfloat16)
    mean_w[0], mean_w[1] = high, low
    hbm, smem = pl.BlockSpec(memory_space=pl.ANY), pl.BlockSpec(memory_space=pltpu.SMEM)
    dma, VM = pltpu.SemaphoreType.DMA, pltpu.VMEM
    masks = [VM((14, 8, LON), F32)]
    return pl.pallas_call(
        kernel,
        name="wave_step",
        out_shape=jax.ShapeDtypeStruct(spectrum.shape, F32),
        in_specs=[hbm, hbm, smem, smem, hbm, hbm, hbm, hbm, hbm, hbm],
        out_specs=hbm,
        scratch_shapes=[
            VM((SIDE, 16, LON), F32), VM((SIDE, 16, LON), F32), VM((SIDE, 8, 128), F32), VM((SIDE, 8, 128), F32),
            VM((ROWS, LON), jnp.int32), VM((2, 48, 128), F32), *masks, VM((2, 8, LON), jnp.int32), *masks * 4,
            VM((2, 14, 8, 8, 128), F32), VM((2, 14, 8, 8, 128), F32), VM((14, 8, 8, 128), F32),
            VM((2, 2, NSUB, 16, LON), F32), VM((2, 2, NSUB, 8, 128), F32),
            VM((ROWS, MSG, 128), BF16), VM((CHUNKS, GROUPS, MSG, 128), BF16),
            VM((CHUNKS, GROUPS, MSG, 128), BF16), VM((ROWS, MSG, 128), BF16),
            VM((K, K), BF16), VM((K, K), BF16), VM((K, K), BF16), VM((HID, K), BF16), VM((K, HID), BF16),
            VM((NFREQ, NDIR), F32), VM((NFREQ, NDIR), F32), VM((K, 128), F32), VM((K, 128), F32),
            VM((HID, LON), BF16), VM((8, LON), F32), VM((16 * GROUPS, 128), F32), VM((128, LON), BF16),
            VM((16 * GROUPS, 128), F32),
            dma((CHUNKS, 4)), dma((4,)), dma((2, 2)), dma((2, 2)), dma((2,)), dma((2,)), dma((3,)),
            dma((CHUNKS,)), dma((CHUNKS,)), dma((CHUNKS,)), dma((CHUNKS,)), dma((1,)),
        ],
        compiler_params=pltpu.CompilerParams(
            collective_id=0, has_side_effects=True, vmem_limit_bytes=60 * 1024 * 1024
        ),
    )(spectrum, sea_mask, sub_counts, jnp.asarray(speed), jnp.asarray(angle_tables()), mix_in, mix_out,
      jnp.asarray(mean_w), growth, damping)


def solution(mesh):
    return jax.shard_map(
        local,
        mesh=mesh,
        in_specs=(
            P("comp", None, "lat", None),
            P("lat", None),
            P("lat", None),
            P("lat"),
            P("comp"),
            P(),
            P(),
            P(),
            P(),
        ),
        out_specs=P("comp", None, "lat", None),
        check_vma=False,
    )
```

time: 127 us -> 104 us (0.82)
  Pallas kernels: 114 us -> 95.7 us
  local copies, waits for them, and re-layouts: 11.9 us -> 7.32 us
    pallas_call x1, Pallas kernels: 114 us -> 95.7 us  [local(): pl.pallas_call(kernel, name='wave_step', out_shape=jax.ShapeDtypeStruct(s...]
    broadcast_in_dim x2 -> x0, local copies, waits for them, and re-layouts: 2.06 us -> none  [the longest x1 1.04 us: local(): gain = jnp.broadcast_to(0.5 * ordered(growth)[:, None], (K, 128))]
    unnamed x3 -> x1, local copies, waits for them, and re-layouts: 8.93 us -> 7.32 us
where the time goes in v1:
time: 104 us
  Pallas kernels  95.7 us (92%)
  local copies, waits for them, and re-layouts  7.32 us (7%)
    pallas_call x1, Pallas kernels, local(): pl.pallas_call(kernel, name='wave_step', out_shape=jax.ShapeDtypeStruct(s...  95.7 us
    unnamed x1, local copies, waits for them, and re-layouts  7.32 us

profile of v1, /device:TPU:1, one launch (start us, length us, event | category | flops | bytes accessed | tf_op | source)
XLA Modules:
  0.0 103.7 jit_solution(13470044853514201034)
XLA Ops:
  0.7 95.7 %wave_step.1 = f32[1,36,96,512]{3,2,1,0:T(8,128)} custom-call(f32[1,36,96,512]{3,2,1,0:T(8,128)} %spec.1, s32[96,512]{1,0:T(8,128)} %mask.1, s32[1]{0:T(128)S(6)} %copy.12.counts, f32[32]{0:T(128)} %constant.6.clone.speed, f32[2,48,128]{2,1,0:T(8,128)} %constant.7.clone.table, bf16[1152,1152]{1,0:T(8,128)(2,1)} %w_in.1, bf16[1152,1152]{1,0:T(8,128)(2,1)} %w_out.1, ...), custom_call_target="tpu_custom_call" | custom-call | tf_op jit(solution)/shard_map/wave_step/pallas_call | solution.py:560
  96.4 7.3 %copy.13 = f32[1,36,96,512]{3,2,1,0:T(8,128)} copy(f32[1,36,96,512]{3,2,1,0:T(8,128)} %wave_step.1) | data formatting | bytes 14155776

commit v2 on v1

--- a/solution.py
+++ b/solution.py
@@ -12,14 +12,15 @@
 MESH = pl.DeviceIdType.MESH
 F32, BF16 = jnp.float32, jnp.bfloat16
 NSUB = 4
+VMEM = 67_043_328
 NDIR, NFREQ, ROWS, LON = 36, 32, 96, 512
 K = NDIR * NFREQ
 GROUPS = 32
 CHUNKS = ROWS // GROUPS
 HALO = 4
-EDGE = 8
-SIDE = ROWS + 2 * EDGE
 PHASES = (1, 2, 0)
+PIECES = ((32, 16), (48, 16), (64, 32), (0, 32))
+FIELD_BYTES = ROWS * (2 * 16 * LON + 2 * 8 * 128) * 4
 MAIN = 32
 MSG = 4 * MAIN + 16
 HID = 1184
@@ -28,7 +29,6 @@
 BLOCK = 8
 
 LATIN = [((i + dy) % 4, dy) for i in range(4) for dy in (1, 3, 2, 0) if ((i + dy) % 4, dy) != (0, 0)]
-ORDER = [(dz, dy, dc) for dz, dy in LATIN for dc in (0, 1)] + [(0, 0, 1)]
 
 
 def direction(quadrant, place):
@@ -57,23 +57,18 @@
     return NDIR * freq + turn
 
 
-def first_row(side, q):
-    return EDGE + q * GROUPS + (EDGE if q else 0) if side == 0 else q * GROUPS + (EDGE if q == 2 else 0)
-
-
 def kernel(
     spec, mask, counts, speed, table, w_in, w_out, mean_w, growth, damping,
-    out,
-    fp, fm, lp, lm, mk, tb, msk, mh, ox, oxm, oy, oym, oxl, oyl, ml, flow, flow_l,
+    fp, fm, lp, lm,
+    run, run_l, mk, tb, msk, mh, ox, oxm, oy, oym, oxl, oyl, ml, flow, flow_l,
     pb, rm, ib, ri, win, wout, perm, wi, wo, gr, dp, gain, damp, sq, hq, lf, rl, tl,
     in_sem, small_sem, halo_send, halo_recv, mask_send, mask_recv, w_sem,
-    send_sem, recv_sem, back_send, back_recv, out_sem,
+    send_sem, recv_sem, back_send, back_recv,
 ):
     me, lat = lax.axis_index("comp"), lax.axis_index("lat")
     z, y, core = lax.div(me, 8), lax.rem(lax.div(me, 2), 4), lax.rem(me, 2)
-    partners = [
-        (lax.rem(z + dz, 4) * 4 + lax.rem(y + dy, 4)) * 2 + lax.rem(core + dc, 2) for dz, dy, dc in ORDER
-    ]
+    chip = lax.div(me, 2)
+    others = [lax.rem(z + dz, 4) * 4 + lax.rem(y + dy, 4) for dz, dy in LATIN]
     fields, lefts = (fp, fm), (lp, lm)
 
     small = [
@@ -83,51 +78,49 @@
     small[0].start()
     small[1].start()
 
-    spans = {1: ((24, 40), (32, 40)), 2: ((64, 32), (64, 32)), 0: ((0, 32), (0, 32))}
-
-    def landing(side, q):
-        row, rows = spans[q][side]
-        return row, pl.ds(first_row(side, q) - (EDGE if q == 1 and side == 0 else 0), rows), rows
-
-    def load(q):
+    spans = ((24, 32), (56, 40), (0, 24))
+
+    def load(n):
+        rows = pl.ds(*spans[n])
         for quadrant in range(4):
             side, i = divmod(quadrant, 2)
-            row, there, rows = landing(side, q)
             for t in range(8):
                 pltpu.make_async_copy(
-                    spec.at[0, direction(quadrant, t), pl.ds(row, rows)], fields[side].at[there, 8 * i + t, :],
-                    in_sem.at[q, side],
+                    spec.at[0, direction(quadrant, t), rows], fields[side].at[rows, 8 * i + t, :], in_sem.at[n, side]
                 ).start()
             for ct in range(4):
                 pltpu.make_async_copy(
-                    spec.at[0, direction(quadrant, 8), pl.ds(row, rows), pl.ds(128 * ct, 128)],
-                    lefts[side].at[there, 2 * ct + i, :],
-                    in_sem.at[q, 2 + side],
+                    spec.at[0, direction(quadrant, 8), rows, pl.ds(128 * ct, 128)],
+                    lefts[side].at[rows, 2 * ct + i, :],
+                    in_sem.at[n, 2 + side],
                 ).start()
 
-    def loaded(q):
-        for side in range(2):
-            _, there, _ = landing(side, q)
-            for ref, sem in ((fields[side], side), (lefts[side], 2 + side)):
-                pltpu.make_async_copy(ref.at[there], ref.at[there], in_sem.at[q, sem]).wait()
+    def loaded(n):
+        rows = pl.ds(*spans[n])
+        for k, ref in enumerate(fields + lefts):
+            pltpu.make_async_copy(ref.at[rows], ref.at[rows], in_sem.at[n, k]).wait()
+
+    run_ups = {(0, 0): (0, 24), (0, 1): (1, 48), (1, 1): (2, 64)}
+    halo_slot = (3, 4)
+    load(0)
+
+    barrier = pltpu.get_barrier_semaphore()
+    for other in others:
+        for c in range(2):
+            pl.semaphore_signal(barrier, inc=1, device_id=(2 * other + c, lat), device_id_type=MESH)
+    pl.semaphore_signal(barrier, inc=1, device_id=(2 * chip + 1 - core, lat), device_id_type=MESH)
+    inner_low, inner_high = lat > 0, lat < 3
+
+    @pl.when(inner_low)
+    def _():
+        pl.semaphore_signal(barrier, inc=1, device_id=(me, lat - 1), device_id_type=MESH)
+
+    @pl.when(inner_high)
+    def _():
+        pl.semaphore_signal(barrier, inc=1, device_id=(me, lat + 1), device_id_type=MESH)
 
     load(1)
-
-    barrier = pltpu.get_barrier_semaphore()
-    for partner in partners:
-        pl.semaphore_signal(barrier, inc=1, device_id=(partner, lat), device_id_type=MESH)
-    inner_low, inner_high = lat > 0, lat < 3
-
-    @pl.when(inner_low)
-    def _():
-        pl.semaphore_signal(barrier, inc=1, device_id=(me, lat - 1), device_id_type=MESH)
-
-    @pl.when(inner_high)
-    def _():
-        pl.semaphore_signal(barrier, inc=1, device_id=(me, lat + 1), device_id_type=MESH)
-
     load(2)
-    load(0)
     w_copies = [
         pltpu.make_async_copy(w_in, win, w_sem.at[0]),
         pltpu.make_async_copy(w_out, wout, w_sem.at[1]),
@@ -186,19 +179,15 @@
         left_down(b)
         return 0
 
-    lax.fori_loop(2, 12, inner_openings, 0)
+    lax.fori_loop(4, 8, inner_openings, 0)
     small[1].wait()
     steps = jnp.full((8, 128), counts[0], jnp.int32)
     rate = jnp.full((8, 128), speed[me], F32) / steps.astype(F32)
 
-    flow[0] = jnp.zeros((2, NSUB, 16, LON), F32)
-    flow_l[0] = jnp.zeros((2, NSUB, 8, 128), F32)
-
     def wide(v):
         return jnp.concatenate([v] * 4, axis=1)
 
-    def propagate(q, side, substep):
-        field, left = fields[side], lefts[side]
+    def propagate(n, side, substep):
         a = jnp.where(steps > substep, rate, 0.0)
         coef = [
             (wide(a * tb[0, pl.ds(16 * side + 8 * g, 8), :]), wide(a * tb[1, pl.ds(16 * side + 8 * g, 8), :]))
@@ -206,27 +195,18 @@
         ]
         coef_l = (a * tb[0, pl.ds(32 + 8 * side, 8), :], a * tb[1, pl.ds(32 + 8 * side, 8), :])
         open_y = oym if side else oy
-        run_up = q == 1 or q == 2 * side
-        first = first_row(side, q) // BLOCK
-        low = first - (1 if run_up and side == 0 else 0)
-        high = first + GROUPS // BLOCK + (1 if run_up and side == 1 else 0)
-        if side == 0:
-            ahead = 0 if q == 0 else -1
-        else:
-            ahead = 0 if q == 2 else 1
-
-        def block(n, carry):
+
+        def block(field, left, base, at, places, carry, source=None):
+            field_in, left_in, base_in = source or (field, left, base)
             flows = list(carry)
-            b = high - 1 - n if side else low + n
-            for step in range(BLOCK):
-                j = BLOCK - 1 - step if side else step
-                i = b * BLOCK + j
-                e = (b + ahead, j)
-                row = (b + ahead, slice(j, j + 1), slice(None))
+            for j in places:
+                i = base + j
+                e = (at, j)
+                row = (at, slice(j, j + 1), slice(None))
                 oy_row = open_y[row]
                 for g in range(2):
                     right = g == side
-                    x = field[i, pl.ds(8 * g, 8), :]
+                    x = field_in[base_in + j, pl.ds(8 * g, 8), :]
                     if substep == 0:
                         x = x * msk[row]
                     o = x * coef[g][0] * (ox if right else oxm)[row]
@@ -234,7 +214,7 @@
                     inflow = pltpu.roll(o, 1 if right else LON - 1, 1)
                     field[i, pl.ds(8 * g, 8), :] = x - o + inflow - p + flows[g]
                     flows[g] = p
-                x = left[i]
+                x = left_in[base_in + j]
                 if substep == 0:
                     x = x * ml[e]
                 o = x * coef_l[0] * oxl[(side, *e)]
@@ -248,18 +228,36 @@
                 flows[2] = p
             return tuple(flows)
 
-        slot = 0 if run_up else 1
-        start = (flow[slot, side, substep, 0:8], flow[slot, side, substep, 8:16], flow_l[slot, side, substep])
-        end = lax.fori_loop(0, high - low, block, start)
-        if q == 1:
-            flow[1, side, substep, 0:8] = end[0]
-            flow[1, side, substep, 8:16] = end[1]
-            flow_l[1, side, substep] = end[2]
-
-    def passes(q):
+        first, rows = PIECES[n]
+        low, high = first // BLOCK, (first + rows) // BLOCK
+        edge = 3 - side
+        if n == edge or (n, side) in run_ups:
+            slot = halo_slot[side] if n == edge else run_ups[n, side][0]
+            zero = jnp.zeros((8, LON), F32)
+            start = (zero, zero, jnp.zeros((8, 128), F32))
+            places = range(HALO - 1, -1, -1) if side else range(HALO, BLOCK)
+            source = None
+            if substep == 0 and n != edge:
+                source = (fields[side], lefts[side], run_ups[n, side][1])
+            start = block(run.at[slot], run_l.at[slot], 0, high + 1 if side else low, places, start, source)
+        else:
+            start = (flow[side, substep, 0:8], flow[side, substep, 8:16], flow_l[side, substep])
+
+        def main(k, carry):
+            b = high - 1 - k if side else low + k
+            places = range(BLOCK - 1, -1, -1) if side else range(BLOCK)
+            return block(fields[side], lefts[side], b * BLOCK, b + 1, places, carry)
+
+        end = lax.fori_loop(0, high - low, main, start)
+        if n == 0 or (n == 1 and side == 0):
+            flow[side, substep, 0:8] = end[0]
+            flow[side, substep, 8:16] = end[1]
+            flow_l[side, substep] = end[2]
+
+    def passes(n):
         for substep in range(NSUB):
             for side in range(2):
-                propagate(q, side, substep)
+                propagate(n, side, substep)
 
     def mask_copy(up):
         return pltpu.make_async_remote_copy(
@@ -273,28 +271,64 @@
 
     def halo_copies(up):
         side = 0 if up else 1
-        src, dst = (SIDE - HALO, EDGE - HALO) if up else (0, SIDE - EDGE)
+        src, dst = (ROWS - HALO, HALO) if up else (0, 0)
         return [
             pltpu.make_async_remote_copy(
-                ref.at[pl.ds(src, HALO)], ref.at[pl.ds(dst, HALO)], halo_send.at[side, i], halo_recv.at[side, i],
+                ref.at[pl.ds(src, HALO)], to.at[halo_slot[side], pl.ds(dst, HALO)],
+                halo_send.at[side, i], halo_recv.at[side, i],
                 device_id=(me, lat + 1 if up else lat - 1), device_id_type=MESH,
             )
-            for i, ref in enumerate((fields[side], lefts[side]))
+            for i, (ref, to) in enumerate(((fields[side], run), (lefts[side], run_l)))
         ]
 
     def edge_copies(up):
         return [mask_copy(up), *halo_copies(up)]
 
-    for side, at in ((0, 0), (1, SIDE - HALO)):
-        fields[side][pl.ds(at, HALO)] = jnp.zeros((HALO, 16, LON), F32)
-        lefts[side][pl.ds(at, HALO)] = jnp.zeros((HALO, 8, 128), F32)
-
+    loaded(0)
+    passes(0)
+    neighbours = jnp.where(inner_low, 1, 0) + jnp.where(inner_high, 1, 0)
+    pl.semaphore_wait(barrier, 2 * len(LATIN) + 1 + neighbours)
+
+    def points(first, rows):
+        def row(j, _):
+            r = first + j
+            for ct in range(4):
+                cols = pl.ds(128 * ct, 128)
+                pb[r, pl.ds(MAIN * ct, 16), :] = fp[r, :, cols].astype(BF16)
+                pb[r, pl.ds(MAIN * ct + 16, 16), :] = fm[r, :, cols].astype(BF16)
+            pb[r, pl.ds(4 * MAIN, 16), :] = jnp.concatenate([lp[r], lm[r]], axis=0).astype(BF16)
+            return 0
+
+        lax.fori_loop(0, rows, row, 0)
+
+    def send_copy(q, to, c):
+        return pltpu.make_async_remote_copy(
+            pb.at[q * GROUPS + 16 * c + to], rm.at[q, me], send_sem.at[q], recv_sem.at[q],
+            device_id=(2 * to + c, lat), device_id_type=MESH,
+        )
+
+    def back_copy(q, to, c):
+        return pltpu.make_async_remote_copy(
+            ib.at[q, 2 * to + c], ri.at[q * GROUPS + 16 * core + chip], back_send.at[q], back_recv.at[q],
+            device_id=(2 * to + c, lat), device_id_type=MESH,
+        )
+
+    def send(q, c):
+        for other in others:
+            send_copy(q, other, c).start()
+
+        @pl.when(core != c)
+        def _():
+            send_copy(q, chip, c).start()
+
+        @pl.when(core == c)
+        def _():
+            pltpu.make_async_copy(pb.at[q * GROUPS + 16 * c + chip], rm.at[q, me], recv_sem.at[q]).start()
+
+    points(*PIECES[0])
+    send(1, 0)
     loaded(1)
-    passes(1)
-    neighbours = jnp.where(inner_low, 1, 0) + jnp.where(inner_high, 1, 0)
-    pl.semaphore_wait(barrier, len(ORDER) + neighbours)
     loaded(2)
-    loaded(0)
 
     @pl.when(inner_high)
     def _():
@@ -306,39 +340,11 @@
         for copy in edge_copies(False):
             copy.start()
 
-    def points(q):
-        low, high = first_row(0, q), first_row(1, q)
-
-        def row(j, _):
-            r = q * GROUPS + j
-            for ct in range(4):
-                cols = pl.ds(128 * ct, 128)
-                pb[r, pl.ds(MAIN * ct, 16), :] = fp[low + j, :, cols].astype(BF16)
-                pb[r, pl.ds(MAIN * ct + 16, 16), :] = fm[high + j, :, cols].astype(BF16)
-            pb[r, pl.ds(4 * MAIN, 16), :] = jnp.concatenate([lp[low + j], lm[high + j]], axis=0).astype(BF16)
-            return 0
-
-        lax.fori_loop(0, GROUPS, row, 0)
-
-    def send_copy(q, partner):
-        return pltpu.make_async_remote_copy(
-            pb.at[q * GROUPS + partner], rm.at[q, me], send_sem.at[q], recv_sem.at[q],
-            device_id=(partner, lat), device_id_type=MESH,
-        )
-
-    def back_copy(q, partner):
-        return pltpu.make_async_remote_copy(
-            ib.at[q, partner], ri.at[q * GROUPS + me], back_send.at[q], back_recv.at[q],
-            device_id=(partner, lat), device_id_type=MESH,
-        )
-
-    def send(q):
-        points(q)
-        for partner in partners:
-            send_copy(q, partner).start()
-        pltpu.make_async_copy(pb.at[q * GROUPS + me], rm.at[q, me], recv_sem.at[q]).start()
-
-    send(1)
+    lax.fori_loop(2, 4, inner_openings, 0)
+    lax.fori_loop(8, 12, inner_openings, 0)
+    passes(1)
+    points(*PIECES[1])
+    send(1, 1)
 
     def select_columns(i, _):
         rows = pl.ds(pl.multiple_of(i * 384, 384), 384)
@@ -361,11 +367,6 @@
 
         lax.fori_loop(0, K // 128, tile, 0)
 
-    for copy in w_copies:
-        copy.wait()
-    build(True)
-    lax.fori_loop(0, 3, select_columns, 0)
-
     @pl.when(inner_low)
     def _():
         for copy in edge_copies(True):
@@ -389,14 +390,14 @@
     @pl.when(jnp.logical_not(inner_low))
     def _():
         mh[0] = jnp.zeros((8, LON), jnp.int32)
-        fp[pl.ds(HALO, HALO)] = jnp.zeros((HALO, 16, LON), F32)
-        lp[pl.ds(HALO, HALO)] = jnp.zeros((HALO, 8, 128), F32)
+        run[halo_slot[0], pl.ds(HALO, HALO)] = jnp.zeros((HALO, 16, LON), F32)
+        run_l[halo_slot[0], pl.ds(HALO, HALO)] = jnp.zeros((HALO, 8, 128), F32)
 
     @pl.when(jnp.logical_not(inner_high))
     def _():
         mh[1] = jnp.zeros((8, LON), jnp.int32)
-        fm[pl.ds(SIDE - EDGE, HALO)] = jnp.zeros((HALO, 16, LON), F32)
-        lm[pl.ds(SIDE - EDGE, HALO)] = jnp.zeros((HALO, 8, 128), F32)
+        run[halo_slot[1], pl.ds(0, HALO)] = jnp.zeros((HALO, 16, LON), F32)
+        run_l[halo_slot[1], pl.ds(0, HALO)] = jnp.zeros((HALO, 8, 128), F32)
 
     msk[0] = mh[0].astype(F32)
     msk[13] = mh[1].astype(F32)
@@ -410,9 +411,16 @@
         open_down(b)
         left_down(b)
 
-    for q in PHASES[1:]:
-        passes(q)
-        send(q)
+    for n, q in ((2, 2), (3, 0)):
+        passes(n)
+        points(*PIECES[n])
+        send(q, 0)
+        send(q, 1)
+
+    for copy in w_copies:
+        copy.wait()
+    build(True)
+    lax.fori_loop(0, 3, select_columns, 0)
 
     build(False)
     lax.fori_loop(0, 3, select_rows, 0)
@@ -476,44 +484,19 @@
                 tl[pl.ds(2 * ct + i, 64, stride=8), :] = result[64 * i : 64 * i + 64]
         ib[q, :, pl.ds(4 * MAIN, 16), :] = tl[...].astype(BF16).reshape(GROUPS, 16, 128)
 
-    def chunk(q, _):
+    def chunk(q):
         pltpu.make_async_copy(rm.at[q], rm.at[q], recv_sem.at[q]).wait()
         sources(q)
-        for partner in partners:
-            back_copy(q, partner).start()
-        pltpu.make_async_copy(ib.at[q, me], ri.at[q * GROUPS + me], back_recv.at[q]).start()
-        return 0
+        for c in range(2):
+            for other in others:
+                back_copy(q, other, c).start()
+        back_copy(q, chip, 1 - core).start()
+        pltpu.make_async_copy(ib.at[q, me], ri.at[q * GROUPS + 16 * core + chip], back_recv.at[q]).start()
 
     for q in PHASES:
-        chunk(q, 0)
-
-    def store_copies(q):
-        first = q * GROUPS
-        copies = []
-        for quadrant in range(4):
-            side = quadrant // 2
-            src, here = fields[side], pl.ds(first_row(side, q), GROUPS)
-            for t in range(8):
-                copies.append(
-                    pltpu.make_async_copy(
-                        src.at[here, 8 * (quadrant % 2) + t, :],
-                        out.at[0, direction(quadrant, t), pl.ds(first, GROUPS), :],
-                        out_sem.at[0],
-                    )
-                )
-            src = lefts[side]
-            for ct in range(4):
-                copies.append(
-                    pltpu.make_async_copy(
-                        src.at[here, 2 * ct + quadrant % 2, :],
-                        out.at[0, direction(quadrant, 8), pl.ds(first, GROUPS), pl.ds(128 * ct, 128)],
-                        out_sem.at[0],
-                    )
-                )
-        return copies
+        chunk(q)
 
     for q in PHASES:
-        low, high = first_row(0, q), first_row(1, q)
         pltpu.make_async_copy(
             ri.at[pl.ds(q * GROUPS, GROUPS)], ri.at[pl.ds(q * GROUPS, GROUPS)], back_recv.at[q]
         ).wait()
@@ -521,28 +504,36 @@
         def rows(b, _):
             block_at = q * (GROUPS // BLOCK) + b + 1
             for j in range(BLOCK):
-                here = b * BLOCK + j
-                r = q * GROUPS + here
+                r = q * GROUPS + b * BLOCK + j
                 for ct in range(4):
                     cols = pl.ds(128 * ct, 128)
                     sea = msk[block_at, j : j + 1, cols]
-                    fp[low + here, :, cols] += ri[r, pl.ds(MAIN * ct, 16), :].astype(F32) * sea
-                    fm[high + here, :, cols] += ri[r, pl.ds(MAIN * ct + 16, 16), :].astype(F32) * sea
+                    fp[r, :, cols] += ri[r, pl.ds(MAIN * ct, 16), :].astype(F32) * sea
+                    fm[r, :, cols] += ri[r, pl.ds(MAIN * ct + 16, 16), :].astype(F32) * sea
                 left = ri[r, pl.ds(4 * MAIN, 16), :].astype(F32)
-                lp[low + here] += left[0:8] * ml[block_at, j]
-                lm[high + here] += left[8:16] * ml[block_at, j]
+                lp[r] += left[0:8] * ml[block_at, j]
+                lm[r] += left[8:16] * ml[block_at, j]
             return 0
 
         lax.fori_loop(0, GROUPS // BLOCK, rows, 0)
-        for copy in store_copies(q):
-            copy.start()
-
-    sent = pb.at[pl.ds(0, len(ORDER))]
+
+    sent = pb.at[pl.ds(0, 2 * len(LATIN) + 1)]
     for q in range(CHUNKS):
         pltpu.make_async_copy(sent, sent, send_sem.at[q]).wait()
         pltpu.make_async_copy(sent, sent, back_send.at[q]).wait()
-    for ref in (fp.at[pl.ds(0, ROWS)], fm.at[pl.ds(0, ROWS)], lp.at[pl.ds(0, ROWS)], lm.at[pl.ds(0, ROWS)]):
-        pltpu.make_async_copy(ref, ref, out_sem.at[0]).wait()
+
+
+def store(fp, fm, lp, lm, out, sem):
+    for quadrant in range(4):
+        side, i = divmod(quadrant, 2)
+        for t in range(8):
+            pltpu.make_async_copy((fp, fm)[side].at[:, 8 * i + t, :], out.at[0, direction(quadrant, t)], sem.at[0]).start()
+        for ct in range(4):
+            pltpu.make_async_copy(
+                (lp, lm)[side].at[:, 2 * ct + i, :], out.at[0, direction(quadrant, 8), :, pl.ds(128 * ct, 128)], sem.at[0]
+            ).start()
+    for ref in (fp, fm, lp, lm):
+        pltpu.make_async_copy(ref, ref, sem.at[0]).wait()
 
 
 def local(spectrum, sea_mask, point_index, band_counts, sub_counts, mix_in, mix_out, growth, damping):
@@ -557,31 +548,40 @@
     hbm, smem = pl.BlockSpec(memory_space=pl.ANY), pl.BlockSpec(memory_space=pltpu.SMEM)
     dma, VM = pltpu.SemaphoreType.DMA, pltpu.VMEM
     masks = [VM((14, 8, LON), F32)]
-    return pl.pallas_call(
+    fields = pl.pallas_call(
         kernel,
         name="wave_step",
-        out_shape=jax.ShapeDtypeStruct(spectrum.shape, F32),
+        out_shape=[VM((ROWS, 16, LON), F32)] * 2 + [VM((ROWS, 8, 128), F32)] * 2,
         in_specs=[hbm, hbm, smem, smem, hbm, hbm, hbm, hbm, hbm, hbm],
-        out_specs=hbm,
+        out_specs=[pl.BlockSpec(memory_space=VM)] * 4,
         scratch_shapes=[
-            VM((SIDE, 16, LON), F32), VM((SIDE, 16, LON), F32), VM((SIDE, 8, 128), F32), VM((SIDE, 8, 128), F32),
+            VM((5, BLOCK, 16, LON), F32), VM((5, BLOCK, 8, 128), F32),
             VM((ROWS, LON), jnp.int32), VM((2, 48, 128), F32), *masks, VM((2, 8, LON), jnp.int32), *masks * 4,
             VM((2, 14, 8, 8, 128), F32), VM((2, 14, 8, 8, 128), F32), VM((14, 8, 8, 128), F32),
-            VM((2, 2, NSUB, 16, LON), F32), VM((2, 2, NSUB, 8, 128), F32),
+            VM((2, NSUB, 16, LON), F32), VM((2, NSUB, 8, 128), F32),
             VM((ROWS, MSG, 128), BF16), VM((CHUNKS, GROUPS, MSG, 128), BF16),
             VM((CHUNKS, GROUPS, MSG, 128), BF16), VM((ROWS, MSG, 128), BF16),
             VM((K, K), BF16), VM((K, K), BF16), VM((K, K), BF16), VM((HID, K), BF16), VM((K, HID), BF16),
             VM((NFREQ, NDIR), F32), VM((NFREQ, NDIR), F32), VM((K, 128), F32), VM((K, 128), F32),
             VM((HID, LON), BF16), VM((8, LON), F32), VM((16 * GROUPS, 128), F32), VM((128, LON), BF16),
             VM((16 * GROUPS, 128), F32),
-            dma((CHUNKS, 4)), dma((4,)), dma((2, 2)), dma((2, 2)), dma((2,)), dma((2,)), dma((3,)),
-            dma((CHUNKS,)), dma((CHUNKS,)), dma((CHUNKS,)), dma((CHUNKS,)), dma((1,)),
+            dma((3, 4)), dma((4,)), dma((2, 2)), dma((2, 2)), dma((2,)), dma((2,)), dma((3,)),
+            dma((CHUNKS,)), dma((CHUNKS,)), dma((CHUNKS,)), dma((CHUNKS,)),
         ],
         compiler_params=pltpu.CompilerParams(
-            collective_id=0, has_side_effects=True, vmem_limit_bytes=60 * 1024 * 1024
+            collective_id=0, has_side_effects=True, vmem_limit_bytes=VMEM - FIELD_BYTES
         ),
     )(spectrum, sea_mask, sub_counts, jnp.asarray(speed), jnp.asarray(angle_tables()), mix_in, mix_out,
       jnp.asarray(mean_w), growth, damping)
+    return pl.pallas_call(
+        store,
+        name="wave_store",
+        out_shape=jax.ShapeDtypeStruct(spectrum.shape, F32),
+        in_specs=[pl.BlockSpec(memory_space=VM)] * 4,
+        out_specs=hbm,
+        scratch_shapes=[dma((1,))],
+        compiler_params=pltpu.CompilerParams(vmem_limit_bytes=1024 * 1024),
+    )(*[pltpu.with_memory_space_constraint(field, VM) for field in fields])
 
 
 def solution(mesh):

time: 104 us -> 94.6 us (0.910)
  local copies, waits for them, and re-layouts: 7.32 us -> 0 us
  Pallas kernels: 95.7 us -> 93.6 us
    unnamed x1 -> x0, local copies, waits for them, and re-layouts: 7.32 us -> none
    pallas_call x1 -> x2, Pallas kernels: 95.7 us -> 93.6 us  [the longest x1 90.8 us: local(): pl.pallas_call(kernel, name='wave_step', out_shape=[VM((ROWS, 16, LON), F...]
where the time goes in v2:
time: 94.6 us; the launch traced here: 94.5 us
  Pallas kernels  93.6 us (99%)
    pallas_call x1, Pallas kernels, local(): pl.pallas_call(kernel, name='wave_step', out_shape=[VM((ROWS, 16, LON), F...  90.8 us
    pallas_call x1, Pallas kernels, local(): pl.pallas_call(store, name='wave_store', out_shape=jax.ShapeDtypeStruct(s...  2.86 us

profile of v2, /device:TPU:1, one launch (start us, length us, event | category | flops | bytes accessed | tf_op | source)
XLA Modules:
  0.0 94.5 jit_solution(171440246196715119)
XLA Ops:
  0.7 90.8 %wave_step.1 = (f32[96,16,512]{2,1,0:T(8,128)S(1)}, f32[96,16,512]{2,1,0:T(8,128)S(1)}, f32[96,8,128]{2,1,0:T(8,128)S(1)}, f32[96,8,128]{2,1,0:T(8,128)S(1)}) custom-call(f32[1,36,96,512]{3,2,1,0:T(8,128)} %spec.1, s32[96,512]{1,0:T(8,128)} %mask.1, s32[1]{0:T(128)S(6)} %copy.11.counts, f32[32]{0:T(128)} %constant.6.clone.speed, ...), custom_call_target="tpu_custom_call" | custom-call | tf_op jit(solution)/shard_map/wave_step/pallas_call | solution.py:551
  91.5 2.9 %wave_store.1 = f32[1,36,96,512]{3,2,1,0:T(8,128)} custom-call(f32[96,16,512]{2,1,0:T(8,128)S(1)} %get-tuple-element.9.fp, f32[96,16,512]{2,1,0:T(8,128)S(1)} %get-tuple-element.10.fm, f32[96,8,128]{2,1,0:T(8,128)S(1)} %get-tuple-element.11.lp, f32[96,8,128]{2,1,0:T(8,128)S(1)} %get-tuple-element.12.lm), custom_call_target="tpu_custom_call" | custom-call | tf_op jit(solution)/shard_map/wave_store/pallas_call | solution.py:576

commit v3 on v2

--- a/solution.py
+++ b/solution.py
@@ -19,10 +19,12 @@
 CHUNKS = ROWS // GROUPS
 HALO = 4
 PHASES = (1, 2, 0)
-PIECES = ((32, 16), (48, 16), (64, 32), (0, 32))
+PIECES = (32, 48, 64, 16, 80, 0)
+PIECE = 16
 FIELD_BYTES = ROWS * (2 * 16 * LON + 2 * 8 * 128) * 4
 MAIN = 32
-MSG = 4 * MAIN + 16
+PART = 64
+MSG = 2 * PART + 16
 HID = 1184
 TILE1 = HID // 2
 TILE2 = 512
@@ -100,8 +102,9 @@
         for k, ref in enumerate(fields + lefts):
             pltpu.make_async_copy(ref.at[rows], ref.at[rows], in_sem.at[n, k]).wait()
 
-    run_ups = {(0, 0): (0, 24), (0, 1): (1, 48), (1, 1): (2, 64)}
+    run_ups = {(0, 0): (0, 24), (0, 1): (1, 48), (1, 1): (2, 64), (2, 1): (2, 80), (3, 0): (0, 8)}
     halo_slot = (3, 4)
+    keeps = ((0, 1, 2), (0, 3))
     load(0)
 
     barrier = pltpu.get_barrier_semaphore()
@@ -119,18 +122,11 @@
     def _():
         pl.semaphore_signal(barrier, inc=1, device_id=(me, lat + 1), device_id_type=MESH)
 
-    load(1)
-    load(2)
     w_copies = [
         pltpu.make_async_copy(w_in, win, w_sem.at[0]),
         pltpu.make_async_copy(w_out, wout, w_sem.at[1]),
         pltpu.make_async_copy(mean_w, wi.at[pl.ds(K, HID - K)], w_sem.at[2]),
     ]
-    for copy in w_copies:
-        copy.start()
-    small[2].start()
-    small[3].start()
-
     lane = lax.broadcasted_iota(jnp.int32, (8, 128), 1)
     sub = lax.broadcasted_iota(jnp.int32, (8, 128), 0)
     odd = lax.rem(sub, 2) == 1
@@ -179,7 +175,20 @@
         left_down(b)
         return 0
 
-    lax.fori_loop(4, 8, inner_openings, 0)
+    def first_openings(b, _):
+        open_lon(b)
+        open_up(b)
+        left_lon(b)
+        left_up(b)
+        return 0
+
+    def second_openings(b, _):
+        open_down(b)
+        left_down(b)
+        return 0
+
+    lax.fori_loop(4, 8, first_openings, 0)
+    load(1)
     small[1].wait()
     steps = jnp.full((8, 128), counts[0], jnp.int32)
     rate = jnp.full((8, 128), speed[me], F32) / steps.astype(F32)
@@ -228,9 +237,8 @@
                 flows[2] = p
             return tuple(flows)
 
-        first, rows = PIECES[n]
-        low, high = first // BLOCK, (first + rows) // BLOCK
-        edge = 3 - side
+        low, high = PIECES[n] // BLOCK, (PIECES[n] + PIECE) // BLOCK
+        edge = 5 - side
         if n == edge or (n, side) in run_ups:
             slot = halo_slot[side] if n == edge else run_ups[n, side][0]
             zero = jnp.zeros((8, LON), F32)
@@ -249,15 +257,14 @@
             return block(fields[side], lefts[side], b * BLOCK, b + 1, places, carry)
 
         end = lax.fori_loop(0, high - low, main, start)
-        if n == 0 or (n == 1 and side == 0):
+        if n in keeps[side]:
             flow[side, substep, 0:8] = end[0]
             flow[side, substep, 8:16] = end[1]
             flow_l[side, substep] = end[2]
 
-    def passes(n):
+    def passes(n, side):
         for substep in range(NSUB):
-            for side in range(2):
-                propagate(n, side, substep)
+            propagate(n, side, substep)
 
     def mask_copy(up):
         return pltpu.make_async_remote_copy(
@@ -284,26 +291,20 @@
     def edge_copies(up):
         return [mask_copy(up), *halo_copies(up)]
 
-    loaded(0)
-    passes(0)
-    neighbours = jnp.where(inner_low, 1, 0) + jnp.where(inner_high, 1, 0)
-    pl.semaphore_wait(barrier, 2 * len(LATIN) + 1 + neighbours)
-
-    def points(first, rows):
+    def points(n, side):
         def row(j, _):
-            r = first + j
+            r = PIECES[n] + j
             for ct in range(4):
-                cols = pl.ds(128 * ct, 128)
-                pb[r, pl.ds(MAIN * ct, 16), :] = fp[r, :, cols].astype(BF16)
-                pb[r, pl.ds(MAIN * ct + 16, 16), :] = fm[r, :, cols].astype(BF16)
-            pb[r, pl.ds(4 * MAIN, 16), :] = jnp.concatenate([lp[r], lm[r]], axis=0).astype(BF16)
+                pb[r, pl.ds(PART * side + 16 * ct, 16), :] = fields[side][r, :, pl.ds(128 * ct, 128)].astype(BF16)
+            if side == 1:
+                pb[r, pl.ds(2 * PART, 16), :] = jnp.concatenate([lp[r], lm[r]], axis=0).astype(BF16)
             return 0
 
-        lax.fori_loop(0, rows, row, 0)
-
-    def send_copy(q, to, c):
+        lax.fori_loop(0, PIECE, row, 0)
+
+    def send_copy(q, to, c, part):
         return pltpu.make_async_remote_copy(
-            pb.at[q * GROUPS + 16 * c + to], rm.at[q, me], send_sem.at[q], recv_sem.at[q],
+            pb.at[q * GROUPS + 16 * c + to, part], rm.at[q, me, part], send_sem.at[q], recv_sem.at[q],
             device_id=(2 * to + c, lat), device_id_type=MESH,
         )
 
@@ -313,20 +314,37 @@
             device_id=(2 * to + c, lat), device_id_type=MESH,
         )
 
-    def send(q, c):
+    def send(n, part=pl.ds(0, MSG)):
+        q, c = PIECES[n] // GROUPS, PIECES[n] % GROUPS // PIECE
+
         for other in others:
-            send_copy(q, other, c).start()
+            send_copy(q, other, c, part).start()
 
         @pl.when(core != c)
         def _():
-            send_copy(q, chip, c).start()
+            send_copy(q, chip, c, part).start()
 
         @pl.when(core == c)
         def _():
-            pltpu.make_async_copy(pb.at[q * GROUPS + 16 * c + chip], rm.at[q, me], recv_sem.at[q]).start()
-
-    points(*PIECES[0])
-    send(1, 0)
+            pltpu.make_async_copy(
+                pb.at[q * GROUPS + 16 * c + chip, part], rm.at[q, me, part], recv_sem.at[q]
+            ).start()
+
+    loaded(0)
+    passes(0, 0)
+    points(0, 0)
+    neighbours = jnp.where(inner_low, 1, 0) + jnp.where(inner_high, 1, 0)
+    pl.semaphore_wait(barrier, 2 * len(LATIN) + 1 + neighbours)
+    send(0, pl.ds(0, PART))
+    load(2)
+    for copy in w_copies:
+        copy.start()
+    small[2].start()
+    small[3].start()
+    lax.fori_loop(5, 8, second_openings, 0)
+    passes(0, 1)
+    points(0, 1)
+    send(0, pl.ds(PART, MSG - PART))
     loaded(1)
     loaded(2)
 
@@ -340,11 +358,16 @@
         for copy in edge_copies(False):
             copy.start()
 
-    lax.fori_loop(2, 4, inner_openings, 0)
+    lax.fori_loop(2, 5, inner_openings, 0)
     lax.fori_loop(8, 12, inner_openings, 0)
-    passes(1)
-    points(*PIECES[1])
-    send(1, 1)
+    def piece(n):
+        for side in range(2):
+            passes(n, side)
+            points(n, side)
+        send(n)
+
+    for n in (1, 2, 3):
+        piece(n)
 
     def select_columns(i, _):
         rows = pl.ds(pl.multiple_of(i * 384, 384), 384)
@@ -411,11 +434,8 @@
         open_down(b)
         left_down(b)
 
-    for n, q in ((2, 2), (3, 0)):
-        passes(n)
-        points(*PIECES[n])
-        send(q, 0)
-        send(q, 1)
+    for n in (4, 5):
+        piece(n)
 
     for copy in w_copies:
         copy.wait()
@@ -445,13 +465,18 @@
     lax.fori_loop(0, K // 128, rates, 0)
 
     def sources(q):
-        lf[...] = rm[q, :, pl.ds(4 * MAIN, 16), :].reshape(16 * GROUPS, 128).astype(F32)
+        lf[...] = rm[q, :, pl.ds(2 * PART, 16), :].reshape(16 * GROUPS, 128).astype(F32)
         for ct in range(4):
             for i in range(2):
                 rl[pl.ds(64 * i, 64), pl.ds(128 * ct, 128)] = lf[pl.ds(2 * ct + i, 64, stride=8), :].astype(BF16)
 
+        def both(q, which, ct):
+            return jnp.concatenate(
+                [rm[q, which, pl.ds(PART * side + 16 * ct, 16), :] for side in range(2)], axis=1
+            )
+
         def right_side():
-            main = [rm[q, :, pl.ds(MAIN * ct, MAIN), :].reshape(MAIN * GROUPS, 128) for ct in range(4)]
+            main = [both(q, slice(None), ct).reshape(MAIN * GROUPS, 128) for ct in range(4)]
             return jnp.concatenate([jnp.concatenate(main, axis=1), rl[...]], axis=0)
 
         for part in range(2):
@@ -467,11 +492,13 @@
             dests = TILE2 // MAIN
             transfer = jnp.dot(wo[pl.ds(base, TILE2), :], square, preferred_element_type=F32)
             for ct in range(4):
-                where = (q, pl.ds(i * dests, dests), pl.ds(MAIN * ct, MAIN), slice(None))
-                energy = rm[where].astype(F32).reshape(TILE2, 128)
+                which = pl.ds(i * dests, dests)
+                energy = both(q, which, ct).astype(F32).reshape(TILE2, 128)
                 rate = gain[pl.ds(base, TILE2), :] - damp[pl.ds(base, TILE2), :] * hq[0:1, 128 * ct : 128 * ct + 128]
                 result = energy * rate + 0.125 * transfer[:, 128 * ct : 128 * ct + 128]
-                ib[where] = result.astype(BF16).reshape(dests, MAIN, 128)
+                result = result.astype(BF16).reshape(dests, MAIN, 128)
+                for side in range(2):
+                    ib[q, which, pl.ds(PART * side + 16 * ct, 16), :] = result[:, 16 * side : 16 * side + 16]
             return 0
 
         lax.fori_loop(0, MAIN * GROUPS // TILE2, rows_of, 0)
@@ -482,7 +509,7 @@
             result = rl[:, cols].astype(F32) * rate + 0.125 * transfer[:, cols]
             for i in range(2):
                 tl[pl.ds(2 * ct + i, 64, stride=8), :] = result[64 * i : 64 * i + 64]
-        ib[q, :, pl.ds(4 * MAIN, 16), :] = tl[...].astype(BF16).reshape(GROUPS, 16, 128)
+        ib[q, :, pl.ds(2 * PART, 16), :] = tl[...].astype(BF16).reshape(GROUPS, 16, 128)
 
     def chunk(q):
         pltpu.make_async_copy(rm.at[q], rm.at[q], recv_sem.at[q]).wait()
@@ -508,9 +535,9 @@
                 for ct in range(4):
                     cols = pl.ds(128 * ct, 128)
                     sea = msk[block_at, j : j + 1, cols]
-                    fp[r, :, cols] += ri[r, pl.ds(MAIN * ct, 16), :].astype(F32) * sea
-                    fm[r, :, cols] += ri[r, pl.ds(MAIN * ct + 16, 16), :].astype(F32) * sea
-                left = ri[r, pl.ds(4 * MAIN, 16), :].astype(F32)
+                    fp[r, :, cols] += ri[r, pl.ds(16 * ct, 16), :].astype(F32) * sea
+                    fm[r, :, cols] += ri[r, pl.ds(PART + 16 * ct, 16), :].astype(F32) * sea
+                left = ri[r, pl.ds(2 * PART, 16), :].astype(F32)
                 lp[r] += left[0:8] * ml[block_at, j]
                 lm[r] += left[8:16] * ml[block_at, j]
             return 0

time: 94.6 us -> 93 us (0.983)
  Pallas kernels: 93.6 us -> 92 us
    pallas_call x1, Pallas kernels: 90.8 us -> 89.2 us  [local(): pl.pallas_call(kernel, name='wave_step', out_shape=[VM((ROWS, 16, LON), F...]
where the time goes in v3:
time: 93 us; the launch traced here: 92.9 us
  Pallas kernels  92 us (99%)
    pallas_call x1, Pallas kernels, local(): pl.pallas_call(kernel, name='wave_step', out_shape=[VM((ROWS, 16, LON), F...  89.2 us
    pallas_call x1, Pallas kernels, local(): pl.pallas_call(store, name='wave_store', out_shape=jax.ShapeDtypeStruct(s...  2.86 us

profile of v3, /device:TPU:1, one launch (start us, length us, event | category | flops | bytes accessed | tf_op | source)
XLA Modules:
  0.0 92.9 jit_solution(4323496426198370950)
XLA Ops:
  0.7 89.2 %wave_step.1 = (f32[96,16,512]{2,1,0:T(8,128)S(1)}, f32[96,16,512]{2,1,0:T(8,128)S(1)}, f32[96,8,128]{2,1,0:T(8,128)S(1)}, f32[96,8,128]{2,1,0:T(8,128)S(1)}) custom-call(f32[1,36,96,512]{3,2,1,0:T(8,128)} %spec.1, s32[96,512]{1,0:T(8,128)} %mask.1, s32[1]{0:T(128)S(6)} %copy.11.counts, f32[32]{0:T(128)} %constant.6.clone.speed, ...), custom_call_target="tpu_custom_call" | custom-call | tf_op jit(solution)/shard_map/wave_step/pallas_call | solution.py:578
  89.8 2.9 %wave_store.1 = f32[1,36,96,512]{3,2,1,0:T(8,128)} custom-call(f32[96,16,512]{2,1,0:T(8,128)S(1)} %get-tuple-element.9.fp, f32[96,16,512]{2,1,0:T(8,128)S(1)} %get-tuple-element.10.fm, f32[96,8,128]{2,1,0:T(8,128)S(1)} %get-tuple-element.11.lp, f32[96,8,128]{2,1,0:T(8,128)S(1)} %get-tuple-element.12.lm), custom_call_target="tpu_custom_call" | custom-call | tf_op jit(solution)/shard_map/wave_store/pallas_call | solution.py:603
